TPU v7x, 256 devices: a whole 4x4x8 slice. The times are simulated.
256 devices in a mesh: tok: 4 (over y), smp: 64 (over x, z, core).
Axes of the slice: x: 4, y: 4, z: 8, core: 2. Of those that a mesh axis runs over, the one named last changes fastest.
Arguments:
- row_table: float32 [8, 16384, 384], P('tok', 'smp'), may hold values from -6 to 6
- row_accum: float32 [8, 16384], P('tok', 'smp'), may hold values from 0.0001 to 0.01
- last_step: int32 [8, 16384], P('tok', 'smp'), may hold values from 0 to 47
- step_now: int32 [1], replicated, may hold values from 48 to 63
- row_ids: int32 [8, 64, 64, 2], P('tok', 'smp'), may hold values from 0 to 255, as said below
- row_counts: int32 [8, 64, 64], P('tok', 'smp'), may hold values from 1 to 2, as said below
- sample_slots: int32 [8, 16384], P(None, 'smp'), may hold values from 0 to 127, as said below
- labels: int32 [16384], P('smp'), may hold values 0 or 1
- up_weight: bfloat16 [384, 8, 1536], P('smp', 'tok'), may hold values from -0.3125 to 0.3125
- down_weight: bfloat16 [384, 8, 1536], P('smp', 'tok'), may hold values from -0.15625 to 0.15625
- out_weight: float32 [8, 384], P('tok'), may hold values from -0.3125 to 0.3125
Outputs:
- new_table: float32 [8, 16384, 384], P('tok', 'smp')
- new_accum: float32 [8, 16384], P('tok', 'smp')
- grad_down: float32 [384, 8, 1536], P('smp', 'tok')
- logits: float32 [16384], P('smp')
Inputs may be any that keep to these rules, and one draw needn't show every extreme that they name: The first row_counts[t, o, g] entries of each list are distinct; later entries are padding; every token and owner has a list of 2 valid entries for some group. `row_ids`: row numbers within the owner's shard. `sample_slots`: each slot o * 2 + c names a valid entry c < row_counts[t, o, s // 256]. `last_step`: each row's last step is before step_now.
All inputs are finite; a program needn't handle non-finite values. No bound on the sum of `labels` on one device may be relied on, other than what follows from the above.
Results may differ from a plain program's by a relative error of at most 0.0021.
Values may be sent and summed in bfloat16 or wider, within the bound.
No kernel may reach another device: no remote copies, remote signals or barrier semaphores. Data moves between devices by JAX's collectives and lax.ppermute only.
A program may use at most 64 MiB of HBM per device.

v0:
```python
import math

import jax
import jax.numpy as jnp
import numpy as np
from jax import lax
from jax.experimental import pallas as pl
from jax.experimental.pallas import tpu as pltpu
from jax.sharding import Mesh
from jax.sharding import PartitionSpec as P


decay_log = math.log(0.98)
learn_rate = 0.2
norm_eps = 1e-05
f32 = jnp.float32
bf16 = jnp.bfloat16
f16 = jnp.float16
i32 = jnp.int32


NN = (((1,), (0,)), ((), ()))
NT = (((1,), (1,)), ((), ()))
VM = pl.BlockSpec(memory_space=pltpu.VMEM)
SM = pl.BlockSpec(memory_space=pltpu.SMEM)


def dot(a, b, dims=NN):
    return lax.dot_general(a, b, dims, preferred_element_type=f32)


def split(v):
    hi = v.astype(bf16)
    return hi, (v - hi.astype(f32)).astype(bf16)


def dot2(v, b, dims=NN):
    hi, lo = split(v)
    return dot(hi, b, dims) + dot(lo, b, dims)


def iota(shape, dim):
    return lax.broadcasted_iota(i32, shape, dim)


def call(body, outs, scratch=(), n_in=0, smem=0, flops=0, nbytes=0):
    return pl.pallas_call(
        body,
        out_shape=outs,
        in_specs=[SM] * smem + [VM] * (n_in - smem),
        out_specs=jax.tree.map(lambda _: VM, outs),
        scratch_shapes=list(scratch),
        compiler_params=pltpu.CompilerParams(vmem_limit_bytes=40 * 2**20),
        cost_estimate=pl.CostEstimate(flops=flops, bytes_accessed=nbytes, transcendentals=0),
    )


def sds(shape, dtype=f32):
    return jax.ShapeDtypeStruct(shape, dtype)


def slot_columns(tab, cols):
    groups = tab.shape[1]
    col = iota((1, cols), 1)
    chip, tok, grp, slot = col // 8, (col // 4) % 2, (col // 2) % 2, col % 2
    pick = (iota((groups, cols), 0) == chip * 2 + grp).astype(f32)
    every = lax.dot_general(tab, pick, NN, preferred_element_type=f32, precision=lax.Precision.HIGHEST)
    keep = iota((4, cols), 0) == tok * 2 + slot
    return jnp.sum(jnp.where(keep, every, 0.0), axis=0, keepdims=True), tok, slot


def lookup_body(step_ref, table_ref, last_ref, ids_ref, out_ref):
    toks, rows, width = table_ref.shape
    cols = out_ref.shape[0]
    ids, tok, _ = slot_columns(ids_ref[...].astype(f32), cols)
    ids = ids + tok.astype(f32) * rows
    column = jnp.transpose(jnp.broadcast_to(ids, (8, cols)))[:, 0:1]
    total = jnp.zeros((cols, width), f32)
    for j in range(toks):
        elapsed = (step_ref[0] - last_ref[j : j + 1, :]).astype(f32)
        factor = jnp.exp(elapsed * decay_log)
        hit = iota((cols, rows), 1).astype(f32) + (j * rows) == column
        weights = jnp.where(hit, factor, 0.0)
        total = total + lax.dot_general(
            weights, table_ref[j], NN, preferred_element_type=f32, precision=lax.Precision.HIGHEST
        )
    out_ref[...] = total


def list_targets(slots, half):
    group = (iota(slots.shape, 1) >= half).astype(i32)
    return (slots // 2) * 4 + group * 2 + slots % 2


def own_target(targets, token):
    return jnp.sum(jnp.where(iota(targets.shape, 0) == token, targets, 0), axis=0, keepdims=True)


def forward_body(
    where_ref, own_ref, heads_ref, slots_ref, head_ref, order_ref,
    z_ref, xp_ref, xm_ref, xa_ref, xb_ref,
    normed_in_ref, inv_in_ref, active_ref, slope_ref, up_ref, down_ref, normed_out_ref, inv_out_ref, logit_ref,
    all_ref, total_ref, input_ref,
):
    width, lists = own_ref.shape
    samples = slots_ref.shape[1]
    toks = slots_ref.shape[0] // 2
    head = width // toks
    hidden = z_ref.shape[1]
    part = z_ref.shape[0]
    all_ref[0:part] = z_ref[...]
    all_ref[part : 2 * part] = xp_ref[...]
    all_ref[2 * part : 3 * part] = xm_ref[...]
    all_ref[3 * part : 3 * part + part // 2] = xa_ref[...]
    all_ref[3 * part + part // 2 : 4 * part] = xb_ref[...]
    targets = list_targets(slots_ref[0:toks, :], samples // 2)
    row = iota((lists, samples), 0)
    one_own = (row == own_target(targets, where_ref[0])).astype(bf16)
    own = dot2(own_ref[...], one_own)
    mixed = []
    for t in range(toks):
        one = (row == targets[t : t + 1, :]).astype(bf16)
        mixed.append(dot2(heads_ref[t * head : (t + 1) * head, :], one))
    value = own + jnp.concatenate(mixed, axis=0)
    centre = jnp.mean(value, axis=0, keepdims=True)
    shifted = value - centre
    inverse = lax.rsqrt(jnp.mean(shifted * shifted, axis=0, keepdims=True) + norm_eps)
    normed = shifted * inverse
    normed_in_ref[...] = normed
    inv_in_ref[...] = inverse
    input_ref[...] = jnp.transpose(normed.astype(bf16))
    total_ref[...] = jnp.zeros_like(total_ref)
    rows = all_ref.shape[0]
    order_up = (iota((width, rows), 0) == order_ref[0:1, :]).astype(bf16)
    order_down = (iota((width, rows), 0) == order_ref[1:2, :]).astype(bf16)
    chunk = 256

    @pl.loop(0, hidden // chunk)
    def _(i):
        cols = pl.ds(pl.multiple_of(i * chunk, chunk), chunk)
        block = all_ref[:, cols]
        up = dot(order_up, block).astype(bf16)
        down = dot(order_down, block).astype(bf16)
        up_ref[:, cols] = up
        down_ref[:, cols] = down
        pre = dot(input_ref[...], up)
        cumulative = 0.5 * (1.0 + lax.erf(pre * (1.0 / math.sqrt(2.0))))
        density = jnp.exp(-0.5 * pre * pre) * (1.0 / math.sqrt(2.0 * math.pi))
        active = (pre * cumulative).astype(bf16)
        active_ref[:, cols] = active
        slope_ref[:, cols] = cumulative + pre * density
        total_ref[...] += dot(down, active, NT)

    value = normed_in_ref[...] + total_ref[...]
    centre = jnp.mean(value, axis=0, keepdims=True)
    shifted = value - centre
    inverse = lax.rsqrt(jnp.mean(shifted * shifted, axis=0, keepdims=True) + norm_eps)
    normed = shifted * inverse
    normed_out_ref[...] = normed
    inv_out_ref[...] = inverse
    logit_ref[...] = jnp.sum(normed * head_ref[...], axis=0, keepdims=True)


def norm_back(grad_in, normed, inverse):
    first = jnp.mean(grad_in, axis=0, keepdims=True)
    second = jnp.mean(grad_in * normed, axis=0, keepdims=True)
    return inverse * (grad_in - first - normed * second)


def grad_down_body(
    chip_ref, logit_ref, slots_ref, head_ref, normed_out_ref, inv_out_ref, active_ref,
    grad_sum_ref, grad_out_ref, kept_ref, next_ref, far_ref, last_ref, padded_ref,
):
    toks = slots_ref.shape[0] // 2
    width = head_ref.shape[0]
    labels = slots_ref[toks : toks + 1, :].astype(f32)
    dlogit = jax.nn.sigmoid(logit_ref[...]) - labels
    grad = norm_back(dlogit * head_ref[...], normed_out_ref[...], inv_out_ref[...])
    grad_sum_ref[...] = grad
    rounded = grad.astype(bf16)
    grad_out_ref[...] = jnp.transpose(rounded)
    lines, half = kept_ref.shape
    n_z = lines // 24
    line = iota((4 * lines, width), 0)
    chip_x = chip_ref[0] + line // lines
    chip_z = chip_ref[1] + line % lines // 24
    chip = chip_x % 4 * n_z + chip_z % n_z
    for k in range(2):
        source = chip * 12 + line % 24 - 12 * k
        place = (source == iota((4 * lines, width), 1)) & (line % 24 // 12 == k)
        padded_ref[k] = dot(place.astype(bf16), rounded).astype(bf16)
    chunk = 256

    @pl.loop(0, half // chunk)
    def _(i):
        cols = pl.ds(pl.multiple_of(i * chunk, chunk), chunk)
        more = pl.ds(pl.multiple_of(half + i * chunk, chunk), chunk)
        value = dot(padded_ref[0], active_ref[:, cols]) + dot(padded_ref[1], active_ref[:, more])
        kept_ref[:, cols] = value[0:lines]
        next_ref[:, cols] = value[lines : 2 * lines].astype(bf16)
        far_ref[:, cols] = value[2 * lines : 3 * lines].astype(bf16)
        last_ref[:, cols] = value[3 * lines :].astype(bf16)


def grad_rows_body(
    where_ref, slots_ref, grad_sum_ref, grad_out_ref, slope_ref, up_ref, down_ref, normed_in_ref, inv_in_ref,
    own_ref, back_ref, total_ref,
):
    width, lists = own_ref.shape
    samples = slots_ref.shape[1]
    toks = slots_ref.shape[0] // 2
    head = width // toks
    total_ref[...] = grad_sum_ref[...]
    chunk = 256

    @pl.loop(0, slope_ref.shape[1] // chunk)
    def _(i):
        cols = pl.ds(pl.multiple_of(i * chunk, chunk), chunk)
        grad = dot(grad_out_ref[...], down_ref[:, cols])
        grad_pre = (grad * slope_ref[:, cols]).astype(bf16)
        total_ref[...] += dot(up_ref[:, cols], grad_pre, NT)

    mixed = norm_back(total_ref[...], normed_in_ref[...], inv_in_ref[...])
    targets = list_targets(slots_ref[0:toks, :], samples // 2)
    row = iota((lists, samples), 0)
    one_own = (row == own_target(targets, where_ref[0])).astype(bf16)
    hi, lo = split(mixed)
    own_ref[...] = dot(hi, one_own, NT) + dot(lo, one_own, NT)
    for t in range(toks):
        one = (row == targets[t : t + 1, :]).astype(bf16)
        span = slice(t * head, (t + 1) * head)
        back_ref[span, :] = (dot(hi[span], one, NT) + dot(lo[span], one, NT)).astype(bf16)


def update_body(
    step_ref, table_ref, accum_ref, last_ref, ids_ref, counts_ref, back_ref,
    table_out_ref, accum_out_ref,
):
    toks, rows, _ = table_ref.shape
    cols = back_ref.shape[0]
    ids, tok, slot = slot_columns(ids_ref[...].astype(f32), cols)
    counts = counts_ref[...].astype(f32)
    four = jnp.concatenate([counts[0:1], counts[0:1], counts[1:2], counts[1:2]], axis=0)
    have, _, _ = slot_columns(four, cols)
    valid = slot.astype(f32) < have
    row = iota((rows, cols), 0).astype(f32)
    back = back_ref[...]
    for j in range(toks):
        named = jnp.where((tok == j) & valid, ids, -1.0)
        hit = (row == named).astype(f32)
        grads = dot(hit.astype(bf16), back)
        square = grads * grads
        touched = jnp.max(hit, axis=1, keepdims=True) > 0.0
        flat = jnp.concatenate(
            [last_ref[j : j + 1, :].astype(f32), accum_ref[j : j + 1, :], jnp.zeros((6, rows), f32)], axis=0
        )
        upright = jnp.transpose(flat)
        factor = jnp.exp((step_ref[0].astype(f32) - upright[:, 0:1]) * decay_log)
        accum = upright[:, 1:2] + jnp.mean(square, axis=1, keepdims=True)
        wide = jnp.transpose(jnp.broadcast_to(accum, (rows, 8)))
        accum_out_ref[j : j + 1, :] = wide[0:1, :]
        table = table_ref[j]
        updated = table * factor - learn_rate * grads * lax.rsqrt(accum)
        table_out_ref[j] = jnp.where(touched, updated, table)


def ring(value, axis, size, shift):
    return lax.ppermute(value, axis, [(i, (i + shift) % size) for i in range(size)])


def flip(value, axis, size, bit):
    return lax.ppermute(value, axis, [(i, i ^ bit) for i in range(size)])


def weight_order(x, z, core, n_x, n_z, steps_z, part):
    block = part // n_z
    third = block // 4
    line = np.arange(4 * part)
    section = line // part
    step_x = np.array([0, -1, 1, 2])[section]
    step_z = np.asarray(steps_z)[(line % part) // block]
    inner = line % block
    other = inner // (2 * third)
    is_down = (inner // third) % 2
    r = inner % third
    chip = ((x + step_x + n_x) % n_x) * n_z + (z + step_z + n_z) % n_z
    owner = jnp.where(core == 0, other, 1 - other)
    target = (chip * 2 + owner) * third + r
    return jnp.stack([jnp.where(is_down == 0, target, -1), jnp.where(is_down == 1, target, -1)]).astype(i32)


def on_device(
    row_table, row_accum, last_step, step_now, row_ids, row_counts, sample_slots, labels, up_weight, down_weight, out_weight
):
    n_tok, n_x, n_z = lax.axis_size("tok"), lax.axis_size("x"), lax.axis_size("z")
    _, _, width = row_table.shape
    toks, batch = sample_slots.shape
    groups, capacity = row_ids.shape[2:]
    head = width // toks
    hidden = up_weight.shape[2]
    lists = 2 * groups * capacity
    samples = 2 * batch
    core = lax.axis_index("core")
    token = lax.axis_index("tok") * 2 + core

    ids = row_ids[:, 0].transpose(0, 2, 1).reshape(2 * capacity, groups)
    looked = call(
        lookup_body, sds((lists, width)), n_in=4, smem=1, flops=10**9, nbytes=2 * 10**6
    )(step_now, row_table, last_step, ids)
    sent = looked.astype(f16).reshape(groups, 2 * capacity, width)
    got = lax.all_to_all(sent, ("x", "z", "core"), 0, 0, tiled=True)
    own = got.reshape(lists, width).T
    heads = lax.all_to_all(own.reshape(toks, head, lists), ("tok", "core"), 0, 0, tiled=True)
    heads = heads.reshape(width, lists).astype(f32)
    own = own.astype(f32)

    mine = jnp.concatenate([sample_slots, labels[None], jnp.zeros((toks - 1, batch), i32)], axis=0)
    theirs = flip(mine, "core", 2, 1)
    slots = jnp.where(core == 0, jnp.concatenate([mine, theirs], axis=1), jnp.concatenate([theirs, mine], axis=1))

    both = jnp.concatenate([up_weight, down_weight], axis=0)
    keep = jnp.where(core == 0, both[:, 0], both[:, 1])
    give = jnp.where(core == 0, both[:, 1], both[:, 0])
    piece = jnp.concatenate([keep, flip(give, "core", 2, 1)], axis=0)
    before, after = ring(piece, "z", n_z, 1), ring(piece, "z", n_z, -1)
    pair = jnp.concatenate([before, piece], axis=0)
    three = jnp.concatenate([before, piece, after], axis=0)
    far_before, far_after = ring(three, "z", n_z, 3), ring(pair, "z", n_z, -3)
    line = jnp.concatenate([three, far_before, far_after], axis=0)
    steps_z = (-1, 0, 1, -4, -3, -2, 2, 3)
    part = line.shape[0]
    x_before, x_after = ring(line, "x", n_x, 1), ring(line, "x", n_x, -1)
    far_a = ring(x_before[: part // 2], "x", n_x, 1)
    far_b = ring(x_after[part // 2 :], "x", n_x, -1)
    order = weight_order(lax.axis_index("x"), lax.axis_index("z"), core, n_x, n_z, steps_z, part)

    where = token.reshape(1).astype(i32)
    head_weight = jnp.where(core == 0, out_weight[0], out_weight[1])[:, None]
    full = (samples, hidden)
    normed_in, inv_in, active, slope, up, down, normed_out, inv_out, partial = call(
        forward_body,
        (
            sds((width, samples)), sds((1, samples)), sds(full, bf16), sds(full), sds((width, hidden), bf16),
            sds((width, hidden), bf16), sds((width, samples)), sds((1, samples)), sds((1, samples)),
        ),
        scratch=(
            pltpu.VMEM((4 * part, hidden), bf16), pltpu.VMEM((width, samples), f32), pltpu.VMEM((samples, width), bf16)
        ),
        n_in=11, smem=1, flops=4 * 10**9, nbytes=10**7,
    )(where, own, heads, slots, head_weight, order, line, x_before, x_after, far_a, far_b)
    logits = partial + flip(partial, "core", 2, 1)
    there = [flip(logits, "tok", n_tok, k) for k in (1, 2, 3)]
    logits = (logits + there[0]) + (there[1] + there[2])

    third = width // (n_x * n_z * 2)
    lines = n_z * 4 * third
    block = (lines, hidden // 2)
    chip = jnp.stack([lax.axis_index("x"), lax.axis_index("z")]).astype(i32)
    grad_sum, grad_out, kept, *away = call(
        grad_down_body,
        (sds((width, samples)), sds((samples, width), bf16), sds(block), sds(block, bf16), sds(block, bf16), sds(block, bf16)),
        scratch=(pltpu.VMEM((2, n_x * lines, samples), bf16),),
        n_in=7, smem=1, flops=10**9, nbytes=4 * 10**6,
    )(chip, logits, slots, head_weight, normed_out, inv_out, active)
    come = [ring(v, "x", n_x, k + 1) for k, v in enumerate(away)]
    total = kept + sum(v.astype(f32) for v in come)
    total = [total[k * 4 * third : (k + 1) * 4 * third] for k in range(n_z)]
    for k in range(1, n_z):
        total[k] = ring(total[k], "z", n_z, k)

    own_grads, head_grads = call(
        grad_rows_body,
        (sds((width, lists)), sds((width, lists), bf16)),
        scratch=(pltpu.VMEM((width, samples), f32),),
        n_in=9, smem=1, flops=2 * 10**9, nbytes=8 * 10**6,
    )(where, slots, grad_sum, grad_out, slope, up, down, normed_in, inv_in)
    returned = lax.all_to_all(head_grads.reshape(toks, head, lists), ("tok", "core"), 0, 0, tiled=True)
    list_grads = (own_grads + returned.reshape(width, lists).astype(f32)).T.astype(bf16)
    back = lax.all_to_all(list_grads.reshape(groups, 2 * capacity, width), ("x", "z", "core"), 0, 0, tiled=True)
    new_table, new_accum = call(
        update_body,
        (sds(row_table.shape), sds(row_accum.shape)),
        n_in=7, smem=1, flops=10**9, nbytes=3 * 10**6,
    )(step_now, row_table, row_accum, last_step, ids, row_counts[:, 0], back.reshape(lists, width))

    summed = sum(total[1:], total[0])
    summed = jnp.concatenate([summed[: 2 * third], summed[2 * third :]], axis=1)
    low, high = summed[:third], summed[third:]
    stay, leave = jnp.where(core == 0, low, high), jnp.where(core == 0, high, low)
    come = flip(leave, "core", 2, 1)
    grad_down = jnp.where(core == 0, jnp.stack([stay, come], axis=1), jnp.stack([come, stay], axis=1))
    logits = jnp.where(core == 0, logits[0, :batch], logits[0, batch:])
    return (new_table, new_accum, grad_down, logits)


def solution(mesh):
    devices = mesh.devices.reshape(4, 4, 8, 2)
    wide = Mesh(devices, ("tok", "x", "z", "core"))
    smp = ("x", "z", "core")
    return jax.shard_map(
        on_device,
        mesh=wide,
        in_specs=(
            P("tok", smp, None),
            P("tok", smp),
            P("tok", smp),
            P(),
            P("tok", smp, None, None),
            P("tok", smp, None),
            P(None, smp),
            P(smp),
            P(smp, "tok", None),
            P(smp, "tok", None),
            P("tok", None),
        ),
        out_specs=(P("tok", smp, None), P("tok", smp), P(smp, "tok", None), P(smp)),
        check_vma=False,
    )
```

profile of v0, /device:TPU:2, one launch (start us, length us, event | category | flops | bytes accessed | tf_op | source)
XLA Modules:
  0.0 138.8 jit_solution(11061809333478111220)
XLA Ops:
  0.6 0.8 copy.28
  1.4 0.8 copy.29
  2.3 1.2 collective-permute-done.1
  3.6 5.9 %collective-permute-start.3 = (bf16[24,1536]{1,0:T(8,128)(2,1)S(1)}, bf16[24,1536]{1,0:T(8,128)(2,1)S(1)}, u32[]{:S(2)}, u32[]{:S(2)}) collective-permute-start(bf16[24,1536]{1,0:T(8,128)(2,1)S(1)} %pad_maximum_fusion.2), channel_id=1, source_target_pairs={{0,14},{2,0},{4,2},{6,4},{8,6},{10,8},{12,10},{14,12},{1,15},{3,1}... | collective-permute-start | bytes 221192 | tf_op jit(solution)/shard_map/ppermute | solution.py:268
  9.5 2.0 %collective-permute-done.3 = bf16[24,1536]{1,0:T(8,128)(2,1)S(1)} collective-permute-done((bf16[24,1536]{1,0:T(8,128)(2,1)S(1)}, bf16[24,1536]{1,0:T(8,128)(2,1)S(1)}, u32[]{:S(2)}, u32[]{:S(2)}) %collective-permute-start.3) | collective-permute-done | bytes 73760 | tf_op jit(solution)/shard_map/ppermute | solution.py:268
  11.5 3.6 %collective-permute-done.2 = bf16[24,1536]{1,0:T(8,128)(2,1)S(1)} collective-permute-done((bf16[24,1536]{1,0:T(8,128)(2,1)S(1)}, bf16[24,1536]{1,0:T(8,128)(2,1)S(1)}, u32[]{:S(2)}, u32[]{:S(2)}) %collective-permute-start.2) | collective-permute-done | bytes 73760 | tf_op jit(solution)/shard_map/ppermute | solution.py:268
  15.2 5.1 %collective-permute-start.5 = (bf16[48,1536]{1,0:T(8,128)(2,1)S(1)}, bf16[48,1536]{1,0:T(8,128)(2,1)S(1)}, u32[]{:S(2)}, u32[]{:S(2)}) collective-permute-start(bf16[48,1536]{1,0:T(8,128)(2,1)S(1)} %pad_maximum_fusion.1), channel_id=1, source_target_pairs={{0,10},{2,12},{4,14},{6,0},{8,2},{10,4},{12,6},{14,8},{1,11},{3,13... | collective-permute-start | bytes 442376 | tf_op jit(solution)/shard_map/ppermute | solution.py:268
  20.3 0.7 pad_add_fusion
  21.7 1.1 copy-done
  22.9 0.7 copy-done.3
  23.5 0.7 copy-done.5
  24.2 1.3 shard_map.201
  25.7 0.7 reshape.65
  26.5 6.4 %all-to-all-start = ((f16[64,4,384]{2,1,0:T(4,128)(2,1)}), f16[64,4,384]{2,1,0:T(4,128)(2,1)S(1)}, u32[]{:S(2)}, u32[]{:S(2)}) async-start(f16[64,4,384]{2,1,0:T(4,128)(2,1)} %reshape.65), calls=%async_computation | async-start | bytes 393216 | tf_op jit(solution)/shard_map/all_to_all | solution.py:311
  33.8 1.6 %collective-permute-start.6 = (bf16[192,1536]{1,0:T(8,128)(2,1)S(1)}, bf16[192,1536]{1,0:T(8,128)(2,1)S(1)}, u32[]{:S(2)}, u32[]{:S(2)}) collective-permute-start(bf16[192,1536]{1,0:T(8,128)(2,1)S(1)} %concatenate.37.z_ref), channel_id=1, source_target_pairs={{0,16},{16,32},{32,48},{48,0},{1,17},{17,33},{33,49},{49,1},{2,18}... | collective-permute-start | bytes 1769480 | tf_op jit(solution)/shard_map/ppermute | solution.py:268
  35.7 7.5 %all-to-all-done = f16[64,4,384]{2,1,0:T(4,128)(2,1)S(1)} async-done(((f16[64,4,384]{2,1,0:T(4,128)(2,1)}), f16[64,4,384]{2,1,0:T(4,128)(2,1)S(1)}, u32[]{:S(2)}, u32[]{:S(2)}) %all-to-all-start) | async-done | bytes 196640 | tf_op jit(solution)/shard_map/all_to_all | solution.py:311
  43.3 0.9 copy.27
  44.1 4.5 %all-to-all-start.1 = ((f16[8,48,256]{2,1,0:T(8,128)(2,1)}), f16[8,48,256]{2,1,0:T(8,128)(2,1)S(1)}, u32[]{:S(2)}, u32[]{:S(2)}) async-start(f16[8,48,256]{2,1,0:T(8,128)(2,1)} %bitcast.11), calls=%async_computation.1 | async-start | bytes 393216 | tf_op jit(solution)/shard_map/all_to_all | solution.py:313
  48.6 2.0 %collective-permute-done.7.xm_ref = bf16[192,1536]{1,0:T(8,128)(2,1)S(1)} collective-permute-done((bf16[192,1536]{1,0:T(8,128)(2,1)S(1)}, bf16[192,1536]{1,0:T(8,128)(2,1)S(1)}, u32[]{:S(2)}, u32[]{:S(2)}) %collective-permute-start.7) | collective-permute-done | bytes 589856 | tf_op jit(solution)/shard_map/ppermute | solution.py:268
  51.4 0.7 slice.84
  52.1 1.4 collective-permute-start.8
  53.5 1.0 bitcast_convert_fusion.1.own_ref
  54.5 0.9 all-to-all-done.1
  55.5 3.6 %collective-permute-done.9.xb_ref = bf16[96,1536]{1,0:T(8,128)(2,1)S(1)} collective-permute-done((bf16[96,1536]{1,0:T(8,128)(2,1)S(1)}, bf16[96,1536]{1,0:T(8,128)(2,1)S(1)}, u32[]{:S(2)}, u32[]{:S(2)}) %collective-permute-start.9) | collective-permute-done | bytes 294944 | tf_op jit(solution)/shard_map/ppermute | solution.py:268
  59.1 3.2 %collective-permute-done.8.xa_ref = bf16[96,1536]{1,0:T(8,128)(2,1)S(1)} collective-permute-done((bf16[96,1536]{1,0:T(8,128)(2,1)}, bf16[96,1536]{1,0:T(8,128)(2,1)S(1)}, u32[]{:S(2)}, u32[]{:S(2)}) %collective-permute-start.8) | collective-permute-done | bytes 294944 | tf_op jit(solution)/shard_map/ppermute | solution.py:268
  62.3 9.0 %shard_map.202 = (f32[384,512]{1,0:T(8,128)S(1)}, f32[1,512]{1,0:T(1,128)S(1)}, bf16[512,1536]{1,0:T(8,128)(2,1)S(1)}, f32[512,1536]{1,0:T(8,128)S(1)}, bf16[384...) custom-call(s32[1]{0:T(128)} %bitcast.4.where_ref, ...), custom_call_target="tpu_custom_call" | custom-call | flops 4000000000 | bytes 10000000 | tf_op jit(solution)/shard_map/pallas_call | solution.py:340
  71.4 1.1 collective-permute-done.10
  72.5 3.0 %collective-permute-start.13 = (f32[1,512]{1,0:T(1,128)S(1)}, f32[1,512]{1,0:T(1,128)S(1)}, u32[]{:S(2)}, u32[]{:S(2)}) collective-permute-start(f32[1,512]{1,0:T(1,128)S(1)} %add.101), channel_id=1, source_target_pairs={{0,192},{64,128},{128,64},{192,0},{1,193},{65,129},{129,65},{193,1... | collective-permute-start | bytes 6152 | tf_op jit(solution)/shard_map/ppermute | solution.py:272
  75.5 0.6 collective-permute-start.12
  76.7 0.6 collective-permute-done.13
  77.3 3.3 %collective-permute-done.12 = f32[1,512]{1,0:T(1,128)S(1)} collective-permute-done((f32[1,512]{1,0:T(1,128)S(1)}, f32[1,512]{1,0:T(1,128)S(1)}, u32[]{:S(2)}, u32[]{:S(2)}) %collective-permute-start.12) | collective-permute-done | bytes 2080 | tf_op jit(solution)/shard_map/ppermute | solution.py:272
  80.6 4.6 %shard_map.203 = (f32[384,512]{1,0:T(8,128)S(1)}, bf16[512,384]{1,0:T(8,128)(2,1)S(1)}, f32[192,768]{1,0:T(8,128)S(1)}, bf16[192,768]{1,0:T(8,128)(2,1)S(1)}, bf...) custom-call(s32[2]{0:T(128)S(1)} %pad_add_fusion.2.chip_ref, f32[1,512]{1,0:T(1,128)S(1)} %add_add_fusion.1.logit_ref, ...), custom_call_target="tpu_custom_call" | custom-call | flops 1000000000 | bytes 4000000 | tf_op jit(solution)/shard_map/pallas_call | solution.py:359
  85.4 5.0 %collective-permute-start.15 = (bf16[192,768]{1,0:T(8,128)(2,1)S(1)}, bf16[192,768]{1,0:T(8,128)(2,1)S(1)}, u32[]{:S(2)}, u32[]{:S(2)}) collective-permute-start(bf16[192,768]{1,0:T(8,128)(2,1)S(1)} %get-tuple-element.40), channel_id=1, source_target_pairs={{0,32},{16,48},{32,0},{48,16},{1,33},{17,49},{33,1},{49,17},{2,34}... | collective-permute-start | bytes 884744 | tf_op jit(solution)/shard_map/ppermute | solution.py:268
  90.4 6.5 %shard_map.204 = (f32[384,256]{1,0:T(8,128)S(1)}, bf16[384,256]{1,0:T(8,128)(2,1)}) custom-call(s32[1]{0:T(128)} %bitcast.4.where_ref, s32[16,512]{1,0:T(8,128)S(1)} %add_select_fusion.slots_ref, f32[384,512]{1,0:T(8,128)S(1)} %get-tuple-element.27.grad_sum_ref, bf16[512,384]{1,0:T(8,128)(2,1)S(1)} %get-tuple-element.28.grad_out_ref, ...), custom_call_target="tpu_custom_call" | custom-call | flops 2000000000 | bytes 8000000 | tf_op jit(solution)/shard_map/pallas_call | solution.py:371
  96.9 3.4 %all-to-all-start.2 = ((bf16[8,48,256]{2,1,0:T(8,128)(2,1)}), bf16[8,48,256]{2,1,0:T(8,128)(2,1)S(1)}, u32[]{:S(2)}, u32[]{:S(2)}) async-start(bf16[8,48,256]{2,1,0:T(8,128)(2,1)} %bitcast.16), calls=%async_computation.2 | async-start | bytes 393216 | tf_op jit(solution)/shard_map/all_to_all | solution.py:377
  100.3 2.0 %collective-permute-done.16 = bf16[192,768]{1,0:T(8,128)(2,1)S(1)} collective-permute-done((bf16[192,768]{1,0:T(8,128)(2,1)S(1)}, bf16[192,768]{1,0:T(8,128)(2,1)S(1)}, u32[]{:S(2)}, u32[]{:S(2)}) %collective-permute-start.16) | collective-permute-done | bytes 294944 | tf_op jit(solution)/shard_map/ppermute | solution.py:268
  102.5 1.3 collective-permute-start.17
  103.8 2.0 %collective-permute-start.23 = (f32[24,768]{1,0:T(8,128)S(1)}, f32[24,768]{1,0:T(8,128)S(1)}, u32[]{:S(2)}, u32[]{:S(2)}) collective-permute-start(f32[24,768]{1,0:T(8,128)S(1)} %get-tuple-element.51), channel_id=1, source_target_pairs={{0,14},{2,0},{4,2},{6,4},{8,6},{10,8},{12,10},{14,12},{1,15},{3,1}... | collective-permute-start | bytes 221192 | tf_op jit(solution)/shard_map/ppermute | solution.py:268
  105.8 2.0 %collective-permute-start.22 = (f32[24,768]{1,0:T(8,128)S(1)}, f32[24,768]{1,0:T(8,128)S(1)}, u32[]{:S(2)}, u32[]{:S(2)}) collective-permute-start(f32[24,768]{1,0:T(8,128)S(1)} %get-tuple-element.52), channel_id=1, source_target_pairs={{0,12},{2,14},{4,0},{6,2},{8,4},{10,6},{12,8},{14,10},{1,13},{3,15... | collective-permute-start | bytes 221192 | tf_op jit(solution)/shard_map/ppermute | solution.py:268
  107.8 2.8 %collective-permute-start.21 = (f32[24,768]{1,0:T(8,128)S(1)}, f32[24,768]{1,0:T(8,128)S(1)}, u32[]{:S(2)}, u32[]{:S(2)}) collective-permute-start(f32[24,768]{1,0:T(8,128)S(1)} %get-tuple-element.53), channel_id=1, source_target_pairs={{0,10},{2,12},{4,14},{6,0},{8,2},{10,4},{12,6},{14,8},{1,11},{3,13... | collective-permute-start | bytes 221192 | tf_op jit(solution)/shard_map/ppermute | solution.py:268
  110.5 2.2 %collective-permute-start.20 = (f32[24,768]{1,0:T(8,128)S(1)}, f32[24,768]{1,0:T(8,128)S(1)}, u32[]{:S(2)}, u32[]{:S(2)}) collective-permute-start(f32[24,768]{1,0:T(8,128)S(1)} %get-tuple-element.54), channel_id=1, source_target_pairs={{0,8},{2,10},{4,12},{6,14},{8,0},{10,2},{12,4},{14,6},{1,9},{3,11}... | collective-permute-start | bytes 221192 | tf_op jit(solution)/shard_map/ppermute | solution.py:268
  112.8 1.6 %collective-permute-start.19 = (f32[24,768]{1,0:T(8,128)S(1)}, f32[24,768]{1,0:T(8,128)S(1)}, u32[]{:S(2)}, u32[]{:S(2)}) collective-permute-start(f32[24,768]{1,0:T(8,128)S(1)} %get-tuple-element.55), channel_id=1, source_target_pairs={{0,6},{2,8},{4,10},{6,12},{8,14},{10,0},{12,2},{14,4},{1,7},{3,9},... | collective-permute-start | bytes 221192 | tf_op jit(solution)/shard_map/ppermute | solution.py:268
  114.4 4.1 %collective-permute-start.18 = (f32[24,768]{1,0:T(8,128)S(1)}, f32[24,768]{1,0:T(8,128)S(1)}, u32[]{:S(2)}, u32[]{:S(2)}) collective-permute-start(f32[24,768]{1,0:T(8,128)S(1)} %get-tuple-element.56), channel_id=1, source_target_pairs={{0,4},{2,6},{4,8},{6,10},{8,12},{10,14},{12,0},{14,2},{1,5},{3,7},... | collective-permute-start | bytes 221192 | tf_op jit(solution)/shard_map/ppermute | solution.py:268
  118.8 0.7 reshape.69
  119.5 6.6 %all-to-all-start.3 = ((bf16[64,4,384]{2,1,0:T(4,128)(2,1)}), bf16[64,4,384]{2,1,0:T(4,128)(2,1)S(1)}, u32[]{:S(2)}, u32[]{:S(2)}) async-start(bf16[64,4,384]{2,1,0:T(4,128)(2,1)} %reshape.69), calls=%async_computation.3 | async-start | bytes 393216 | tf_op jit(solution)/shard_map/all_to_all | solution.py:379
  127.6 0.7 copy.33
  128.3 8.2 %all-to-all-done.3 = bf16[64,4,384]{2,1,0:T(4,128)(2,1)S(1)} async-done(((bf16[64,4,384]{2,1,0:T(4,128)(2,1)}), bf16[64,4,384]{2,1,0:T(4,128)(2,1)S(1)}, u32[]{:S(2)}, u32[]{:S(2)}) %all-to-all-start.3) | async-done | bytes 196640 | tf_op jit(solution)/shard_map/all_to_all | solution.py:379
  136.6 2.2 %shard_map.205 = (f32[2,256,384]{2,1,0:T(8,128)}, f32[2,256]{1,0:T(2,128)}) custom-call(s32[1]{0:T(128)S(6)} %copy.34.step_ref, f32[2,256,384]{2,1,0:T(8,128)S(1)} %copy-done.1, f32[2,256]{1,0:T(2,128)S(1)} %copy-done.2, s32[2,256]{1,0:T(2,128)S(1)} %copy-done.4, s32[4,64]{1,0:T(4,128)S(1)} %bitcast.34, s32[2,64]{1,0:T(2,128)S(1)} %bitcast.35, ...), custom_call_target="tpu_custom_call" | custom-call | flops 1000000000 | bytes 3000000 | tf_op jit(solution)/shard_map/pallas_call | solution.py:380
  (90 shorter events, 4.9 us)
Async XLA Ops:
  2.2 1.3 collective-permute-start.1
  3.6 7.9 %collective-permute-start.3 = (bf16[24,1536]{1,0:T(8,128)(2,1)S(1)}, bf16[24,1536]{1,0:T(8,128)(2,1)S(1)}, u32[]{:S(2)}, u32[]{:S(2)}) collective-permute-start(bf16[24,1536]{1,0:T(8,128)(2,1)S(1)} %pad_maximum_fusion.2), channel_id=1, source_target_pairs={{0,14},{2,0},{4,2},{6,4},{8,6},{10,8},{12,10},{14,12},{1,15},{3,1}... | collective-permute-start | bytes 221192 | tf_op jit(solution)/shard_map/ppermute | solution.py:268
  9.5 5.6 %collective-permute-start.2 = (bf16[24,1536]{1,0:T(8,128)(2,1)S(1)}, bf16[24,1536]{1,0:T(8,128)(2,1)S(1)}, u32[]{:S(2)}, u32[]{:S(2)}) collective-permute-start(bf16[24,1536]{1,0:T(8,128)(2,1)S(1)} %pad_maximum_fusion.2), channel_id=1, source_target_pairs={{0,2},{2,4},{4,6},{6,8},{8,10},{10,12},{12,14},{14,0},{1,3},{3,5},... | collective-permute-start | bytes 221192 | tf_op jit(solution)/shard_map/ppermute | solution.py:268
  15.1 17.7 %collective-permute-start.4 = (bf16[72,1536]{1,0:T(8,128)(2,1)S(1)}, bf16[72,1536]{1,0:T(8,128)(2,1)S(1)}, u32[]{:S(2)}, u32[]{:S(2)}) collective-permute-start(bf16[72,1536]{1,0:T(8,128)(2,1)S(1)} %pad_maximum_fusion), channel_id=1, source_target_pairs={{0,6},{2,8},{4,10},{6,12},{8,14},{10,0},{12,2},{14,4},{1,7},{3,9},... | collective-permute-start | bytes 663560 | tf_op jit(solution)/shard_map/ppermute | solution.py:268
  15.2 17.6 %collective-permute-start.5 = (bf16[48,1536]{1,0:T(8,128)(2,1)S(1)}, bf16[48,1536]{1,0:T(8,128)(2,1)S(1)}, u32[]{:S(2)}, u32[]{:S(2)}) collective-permute-start(bf16[48,1536]{1,0:T(8,128)(2,1)S(1)} %pad_maximum_fusion.1), channel_id=1, source_target_pairs={{0,10},{2,12},{4,14},{6,0},{8,2},{10,4},{12,6},{14,8},{1,11},{3,13... | collective-permute-start | bytes 442376 | tf_op jit(solution)/shard_map/ppermute | solution.py:268
  21.1 14.6 %collective-permute-start = (s32[16,256]{1,0:T(8,128)S(1)}, s32[16,256]{1,0:T(8,128)S(1)}, u32[]{:S(2)}, u32[]{:S(2)}) collective-permute-start(s32[16,256]{1,0:T(8,128)S(1)} %pad_add_fusion), channel_id=1, source_target_pairs={{0,1},{1,0},{2,3},{3,2},{4,5},{5,4},{6,7},{7,6},{8,9},{9,8},{10,11... | collective-permute-start | bytes 49160 | tf_op jit(solution)/shard_map/ppermute | solution.py:272
  21.7 1.1 copy-start
  22.9 0.7 copy-start.3
  23.5 0.7 copy-start.5
  25.6 9.8 %copy-start.10 = (s32[768]{0:T(1024)S(1)}, s32[768]{0:T(1024)}, u32[]{:S(2)}) copy-start(s32[768]{0:T(1024)} %constant.73.clone) | copy-start | bytes 9220
  25.6 9.8 %copy-start.11 = (s32[768]{0:T(1024)S(1)}, s32[768]{0:T(1024)}, u32[]{:S(2)}) copy-start(s32[768]{0:T(1024)} %constant.72.clone) | copy-start | bytes 9220
  25.6 9.8 %copy-start.12 = (s32[768]{0:T(1024)S(1)}, s32[768]{0:T(1024)}, u32[]{:S(2)}) copy-start(s32[768]{0:T(1024)} %constant.71.clone) | copy-start | bytes 9220
  25.6 9.7 %copy-start.13 = (s32[768]{0:T(1024)S(1)}, s32[768]{0:T(1024)}, u32[]{:S(2)}) copy-start(s32[768]{0:T(1024)} %constant.70.clone) | copy-start | bytes 9220
  25.6 9.7 %copy-start.14 = (s32[768]{0:T(1024)S(1)}, s32[768]{0:T(1024)}, u32[]{:S(2)}) copy-start(s32[768]{0:T(1024)} %constant.69.clone) | copy-start | bytes 9220
  25.6 9.7 %copy-start.16 = (pred[768]{0:T(1024)(128)(4,1)S(1)}, pred[768]{0:T(1024)(128)(4,1)}, u32[]{:S(2)}) copy-start(pred[768]{0:T(1024)(128)(4,1)} %constant.75.clone) | copy-start | bytes 2308
  25.6 9.7 %copy-start.17 = (pred[768]{0:T(1024)(128)(4,1)S(1)}, pred[768]{0:T(1024)(128)(4,1)}, u32[]{:S(2)}) copy-start(pred[768]{0:T(1024)(128)(4,1)} %constant.74.clone) | copy-start | bytes 2308
  25.7 9.8 %copy-start.15 = (f32[2,384]{1,0:T(2,128)S(1)}, f32[2,384]{1,0:T(2,128)}, u32[]{:S(2)}) copy-start(f32[2,384]{1,0:T(2,128)} %param.28) | copy-start | bytes 9220
  25.7 10.0 %copy-start.8 = (s32[8,256]{1,0:T(8,128)S(1)}, s32[8,256]{1,0:T(8,128)}, u32[]{:S(2)}) copy-start(s32[8,256]{1,0:T(8,128)} %param.24) | copy-start | bytes 24580
  25.7 10.0 %copy-start.9 = (s32[256]{0:T(256)S(1)}, s32[256]{0:T(256)}, u32[]{:S(2)}) copy-start(s32[256]{0:T(256)} %param.25) | copy-start | bytes 3076
  26.5 16.7 %all-to-all-start = ((f16[64,4,384]{2,1,0:T(4,128)(2,1)}), f16[64,4,384]{2,1,0:T(4,128)(2,1)S(1)}, u32[]{:S(2)}, u32[]{:S(2)}) async-start(f16[64,4,384]{2,1,0:T(4,128)(2,1)} %reshape.65), calls=%async_computation | async-start | bytes 393216 | tf_op jit(solution)/shard_map/all_to_all | solution.py:311
  33.2 17.4 %collective-permute-start.7 = (bf16[192,1536]{1,0:T(8,128)(2,1)S(1)}, bf16[192,1536]{1,0:T(8,128)(2,1)S(1)}, u32[]{:S(2)}, u32[]{:S(2)}) collective-permute-start(bf16[192,1536]{1,0:T(8,128)(2,1)S(1)} %concatenate.37.z_ref), channel_id=1, source_target_pairs={{0,48},{16,0},{32,16},{48,32},{1,49},{17,1},{33,17},{49,33},{2,50}... | collective-permute-start | bytes 1769480 | tf_op jit(solution)/shard_map/ppermute | solution.py:268
  33.8 17.6 %collective-permute-start.6 = (bf16[192,1536]{1,0:T(8,128)(2,1)S(1)}, bf16[192,1536]{1,0:T(8,128)(2,1)S(1)}, u32[]{:S(2)}, u32[]{:S(2)}) collective-permute-start(bf16[192,1536]{1,0:T(8,128)(2,1)S(1)} %concatenate.37.z_ref), channel_id=1, source_target_pairs={{0,16},{16,32},{32,48},{48,0},{1,17},{17,33},{33,49},{49,1},{2,18}... | collective-permute-start | bytes 1769480 | tf_op jit(solution)/shard_map/ppermute | solution.py:268
  44.1 11.3 %all-to-all-start.1 = ((f16[8,48,256]{2,1,0:T(8,128)(2,1)}), f16[8,48,256]{2,1,0:T(8,128)(2,1)S(1)}, u32[]{:S(2)}, u32[]{:S(2)}) async-start(f16[8,48,256]{2,1,0:T(8,128)(2,1)} %bitcast.11), calls=%async_computation.1 | async-start | bytes 393216 | tf_op jit(solution)/shard_map/all_to_all | solution.py:313
  50.7 8.4 %collective-permute-start.9 = (bf16[96,1536]{1,0:T(8,128)(2,1)S(1)}, bf16[96,1536]{1,0:T(8,128)(2,1)S(1)}, u32[]{:S(2)}, u32[]{:S(2)}) collective-permute-start(bf16[96,1536]{1,0:T(8,128)(2,1)S(1)} %slice.85), channel_id=1, source_target_pairs={{0,48},{16,0},{32,16},{48,32},{1,49},{17,1},{33,17},{49,33},{2,50}... | collective-permute-start | bytes 884744 | tf_op jit(solution)/shard_map/ppermute | solution.py:268
  52.1 10.1 %collective-permute-start.8 = (bf16[96,1536]{1,0:T(8,128)(2,1)}, bf16[96,1536]{1,0:T(8,128)(2,1)S(1)}, u32[]{:S(2)}, u32[]{:S(2)}) collective-permute-start(bf16[96,1536]{1,0:T(8,128)(2,1)} %slice.84), channel_id=1, source_target_pairs={{0,16},{16,32},{32,48},{48,0},{1,17},{17,33},{33,49},{49,1},{2,18}... | collective-permute-start | bytes 884744 | tf_op jit(solution)/shard_map/ppermute | solution.py:268
  71.3 1.3 collective-permute-start.10
  72.5 4.8 %collective-permute-start.13 = (f32[1,512]{1,0:T(1,128)S(1)}, f32[1,512]{1,0:T(1,128)S(1)}, u32[]{:S(2)}, u32[]{:S(2)}) collective-permute-start(f32[1,512]{1,0:T(1,128)S(1)} %add.101), channel_id=1, source_target_pairs={{0,192},{64,128},{128,64},{192,0},{1,193},{65,129},{129,65},{193,1... | collective-permute-start | bytes 6152 | tf_op jit(solution)/shard_map/ppermute | solution.py:272
  75.5 5.1 %collective-permute-start.12 = (f32[1,512]{1,0:T(1,128)S(1)}, f32[1,512]{1,0:T(1,128)S(1)}, u32[]{:S(2)}, u32[]{:S(2)}) collective-permute-start(f32[1,512]{1,0:T(1,128)S(1)} %add.101), channel_id=1, source_target_pairs={{0,128},{64,192},{128,0},{192,64},{1,129},{65,193},{129,1},{193,65... | collective-permute-start | bytes 6152 | tf_op jit(solution)/shard_map/ppermute | solution.py:272
  76.2 4.5 %collective-permute-start.11 = (f32[1,512]{1,0:T(1,128)S(1)}, f32[1,512]{1,0:T(1,128)S(1)}, u32[]{:S(2)}, u32[]{:S(2)}) collective-permute-start(f32[1,512]{1,0:T(1,128)S(1)} %add.101), channel_id=1, source_target_pairs={{0,64},{64,0},{128,192},{192,128},{1,65},{65,1},{129,193},{193,129... | collective-permute-start | bytes 6152 | tf_op jit(solution)/shard_map/ppermute | solution.py:272
  85.3 15.0 %collective-permute-start.14 = (bf16[192,768]{1,0:T(8,128)(2,1)S(1)}, bf16[192,768]{1,0:T(8,128)(2,1)S(1)}, u32[]{:S(2)}, u32[]{:S(2)}) collective-permute-start(bf16[192,768]{1,0:T(8,128)(2,1)S(1)} %get-tuple-element.39), channel_id=1, source_target_pairs={{0,16},{16,32},{32,48},{48,0},{1,17},{17,33},{33,49},{49,1},{2,18}... | collective-permute-start | bytes 884744 | tf_op jit(solution)/shard_map/ppermute | solution.py:268
  85.4 14.9 %collective-permute-start.15 = (bf16[192,768]{1,0:T(8,128)(2,1)S(1)}, bf16[192,768]{1,0:T(8,128)(2,1)S(1)}, u32[]{:S(2)}, u32[]{:S(2)}) collective-permute-start(bf16[192,768]{1,0:T(8,128)(2,1)S(1)} %get-tuple-element.40), channel_id=1, source_target_pairs={{0,32},{16,48},{32,0},{48,16},{1,33},{17,49},{33,1},{49,17},{2,34}... | collective-permute-start | bytes 884744 | tf_op jit(solution)/shard_map/ppermute | solution.py:268
  90.4 11.9 %collective-permute-start.16 = (bf16[192,768]{1,0:T(8,128)(2,1)S(1)}, bf16[192,768]{1,0:T(8,128)(2,1)S(1)}, u32[]{:S(2)}, u32[]{:S(2)}) collective-permute-start(bf16[192,768]{1,0:T(8,128)(2,1)S(1)} %get-tuple-element.41), channel_id=1, source_target_pairs={{0,48},{16,0},{32,16},{48,32},{1,49},{17,1},{33,17},{49,33},{2,50}... | collective-permute-start | bytes 884744 | tf_op jit(solution)/shard_map/ppermute | solution.py:268
  96.9 21.6 %all-to-all-start.2 = ((bf16[8,48,256]{2,1,0:T(8,128)(2,1)}), bf16[8,48,256]{2,1,0:T(8,128)(2,1)S(1)}, u32[]{:S(2)}, u32[]{:S(2)}) async-start(bf16[8,48,256]{2,1,0:T(8,128)(2,1)} %bitcast.16), calls=%async_computation.2 | async-start | bytes 393216 | tf_op jit(solution)/shard_map/all_to_all | solution.py:377
  102.5 10.3 %collective-permute-start.17 = (f32[24,768]{1,0:T(8,128)S(1)}, f32[24,768]{1,0:T(8,128)S(1)}, u32[]{:S(2)}, u32[]{:S(2)}) collective-permute-start(f32[24,768]{1,0:T(8,128)S(1)} %get-tuple-element.50), channel_id=1, source_target_pairs={{0,2},{2,4},{4,6},{6,8},{8,10},{10,12},{12,14},{14,0},{1,3},{3,5},... | collective-permute-start | bytes 221192 | tf_op jit(solution)/shard_map/ppermute | solution.py:268
  103.8 10.6 %collective-permute-start.23 = (f32[24,768]{1,0:T(8,128)S(1)}, f32[24,768]{1,0:T(8,128)S(1)}, u32[]{:S(2)}, u32[]{:S(2)}) collective-permute-start(f32[24,768]{1,0:T(8,128)S(1)} %get-tuple-element.51), channel_id=1, source_target_pairs={{0,14},{2,0},{4,2},{6,4},{8,6},{10,8},{12,10},{14,12},{1,15},{3,1}... | collective-permute-start | bytes 221192 | tf_op jit(solution)/shard_map/ppermute | solution.py:268
  105.8 20.4 %collective-permute-start.22 = (f32[24,768]{1,0:T(8,128)S(1)}, f32[24,768]{1,0:T(8,128)S(1)}, u32[]{:S(2)}, u32[]{:S(2)}) collective-permute-start(f32[24,768]{1,0:T(8,128)S(1)} %get-tuple-element.52), channel_id=1, source_target_pairs={{0,12},{2,14},{4,0},{6,2},{8,4},{10,6},{12,8},{14,10},{1,13},{3,15... | collective-permute-start | bytes 221192 | tf_op jit(solution)/shard_map/ppermute | solution.py:268
  107.8 18.4 %collective-permute-start.21 = (f32[24,768]{1,0:T(8,128)S(1)}, f32[24,768]{1,0:T(8,128)S(1)}, u32[]{:S(2)}, u32[]{:S(2)}) collective-permute-start(f32[24,768]{1,0:T(8,128)S(1)} %get-tuple-element.53), channel_id=1, source_target_pairs={{0,10},{2,12},{4,14},{6,0},{8,2},{10,4},{12,6},{14,8},{1,11},{3,13... | collective-permute-start | bytes 221192 | tf_op jit(solution)/shard_map/ppermute | solution.py:268
  110.5 15.6 %collective-permute-start.20 = (f32[24,768]{1,0:T(8,128)S(1)}, f32[24,768]{1,0:T(8,128)S(1)}, u32[]{:S(2)}, u32[]{:S(2)}) collective-permute-start(f32[24,768]{1,0:T(8,128)S(1)} %get-tuple-element.54), channel_id=1, source_target_pairs={{0,8},{2,10},{4,12},{6,14},{8,0},{10,2},{12,4},{14,6},{1,9},{3,11}... | collective-permute-start | bytes 221192 | tf_op jit(solution)/shard_map/ppermute | solution.py:268
  112.8 13.4 %collective-permute-start.19 = (f32[24,768]{1,0:T(8,128)S(1)}, f32[24,768]{1,0:T(8,128)S(1)}, u32[]{:S(2)}, u32[]{:S(2)}) collective-permute-start(f32[24,768]{1,0:T(8,128)S(1)} %get-tuple-element.55), channel_id=1, source_target_pairs={{0,6},{2,8},{4,10},{6,12},{8,14},{10,0},{12,2},{14,4},{1,7},{3,9},... | collective-permute-start | bytes 221192 | tf_op jit(solution)/shard_map/ppermute | solution.py:268
  114.4 11.8 %collective-permute-start.18 = (f32[24,768]{1,0:T(8,128)S(1)}, f32[24,768]{1,0:T(8,128)S(1)}, u32[]{:S(2)}, u32[]{:S(2)}) collective-permute-start(f32[24,768]{1,0:T(8,128)S(1)} %get-tuple-element.56), channel_id=1, source_target_pairs={{0,4},{2,6},{4,8},{6,10},{8,12},{10,14},{12,0},{14,2},{1,5},{3,7},... | collective-permute-start | bytes 221192 | tf_op jit(solution)/shard_map/ppermute | solution.py:268
  118.6 18.0 %copy-start.1 = (f32[2,256,384]{2,1,0:T(8,128)S(1)}, f32[2,256,384]{2,1,0:T(8,128)}, u32[]{:S(2)}) copy-start(f32[2,256,384]{2,1,0:T(8,128)} %table_ref.3) | copy-start | bytes 2359300
  118.6 18.0 %copy-start.2 = (f32[2,256]{1,0:T(2,128)S(1)}, f32[2,256]{1,0:T(2,128)}, u32[]{:S(2)}) copy-start(f32[2,256]{1,0:T(2,128)} %accum_ref.1) | copy-start | bytes 6148
  118.6 18.0 %copy-start.4 = (s32[2,256]{1,0:T(2,128)S(1)}, s32[2,256]{1,0:T(2,128)}, u32[]{:S(2)}) copy-start(s32[2,256]{1,0:T(2,128)} %last_ref.3) | copy-start | bytes 6148
  118.6 18.0 %copy-start.6 = (s32[2,1,64,2]{2,3,1,0:T(2,128)S(1)}, s32[2,1,64,2]{2,3,1,0:T(2,128)}, u32[]{:S(2)}) copy-start(s32[2,1,64,2]{2,3,1,0:T(2,128)} %param.22) | copy-start | bytes 3076
  118.6 18.0 %copy-start.7 = (s32[2,1,64]{2,1,0:T(1,128)S(1)}, s32[2,1,64]{2,1,0:T(1,128)}, u32[]{:S(2)}) copy-start(s32[2,1,64]{2,1,0:T(1,128)} %param.23) | copy-start | bytes 1540
  119.5 17.0 %all-to-all-start.3 = ((bf16[64,4,384]{2,1,0:T(4,128)(2,1)}), bf16[64,4,384]{2,1,0:T(4,128)(2,1)S(1)}, u32[]{:S(2)}, u32[]{:S(2)}) async-start(bf16[64,4,384]{2,1,0:T(4,128)(2,1)} %reshape.69), calls=%async_computation.3 | async-start | bytes 393216 | tf_op jit(solution)/shard_map/all_to_all | solution.py:379
  126.3 1.3 collective-permute-start.24
where the time goes:
time: 141 us; the launch traced here: 139 us
  starting transfers between devices  61.5 us (44%)
  waiting for transfers between devices  40.2 us (29%)
  Pallas kernels  23.7 us (17%)
  local copies, waits for them, and re-layouts  8.73 us (6%)
  other arithmetic  2.81 us (2%)
  between operations  1.85 us (1%)
    ppermute x18, starting transfers between devices, ring(): lax.ppermute(value, axis, [(i, (i + shift) % size) for i in range(size)])  36.2 us
    ppermute x18, waiting for transfers between devices, ring(): lax.ppermute(value, axis, [(i, (i + shift) % size) for i in range(size)])  16.7 us
    pallas_call x1, Pallas kernels, on_device(): call(forward_body, (sds((width, samples)), sds((1, samples)), sds(full, b...  9 us
    all_to_all x1, waiting for transfers between devices, on_device(): lax.all_to_all(list_grads.reshape(groups, 2 * capacity, width), ('x', 'z'...  8.17 us
    all_to_all x1, waiting for transfers between devices, on_device(): got = lax.all_to_all(sent, ('x', 'z', 'core'), 0, 0, tiled=True)  7.54 us
    ppermute x7, waiting for transfers between devices, flip(): return lax.ppermute(value, axis, [(i, i ^ bit) for i in range(size)])  6.86 us
    all_to_all x1, starting transfers between devices, on_device(): lax.all_to_all(list_grads.reshape(groups, 2 * capacity, width), ('x', 'z'...  6.61 us
    pallas_call x1, Pallas kernels, on_device(): call(grad_rows_body, (sds((width, lists)), sds((width, lists), bf16)), sc...  6.52 us
  transfers between devices with their start and end apart: 29, of which 15 were waited for; matrix products, arithmetic and copies ran while one was open for 5% of the time, Pallas kernels for 6%

commit v1 on v0

--- a/solution.py
+++ b/solution.py
@@ -96,23 +96,47 @@
     return jnp.sum(jnp.where(iota(targets.shape, 0) == token, targets, 0), axis=0, keepdims=True)
 
 
+def order_body(order_ref, chip_ref, z_ref, xa_ref, xb_ref, xc_ref, xd_ref, xe_ref, xf_ref, up_ref, down_ref, place_ref, all_ref):
+    part = z_ref.shape[0]
+    half = part // 2
+    width, hidden = up_ref.shape
+    all_ref[0:part] = z_ref[...]
+    for k, ref in enumerate((xa_ref, xb_ref, xc_ref, xd_ref, xe_ref, xf_ref)):
+        all_ref[part + k * half : part + (k + 1) * half] = ref[...]
+    rows = all_ref.shape[0]
+    order_up = (iota((width, rows), 0) == order_ref[0:1, :]).astype(bf16)
+    order_down = (iota((width, rows), 0) == order_ref[1:2, :]).astype(bf16)
+    chunk = 256
+
+    @pl.loop(0, hidden // chunk)
+    def _(i):
+        cols = pl.ds(pl.multiple_of(i * chunk, chunk), chunk)
+        block = all_ref[:, cols]
+        up_ref[:, cols] = dot(order_up, block).astype(bf16)
+        down_ref[:, cols] = dot(order_down, block).astype(bf16)
+
+    lines = place_ref.shape[1] // 4
+    line = iota((4 * lines, width), 0)
+    pos = line % lines // 24
+    chip_x = (chip_ref[0] + line // lines) % 4
+    chip_z = chip_ref[1] ^ (pos // 2 + pos % 2 * 4)
+    chip = chip_x * (lines // 24) + chip_z
+    for k in range(2):
+        source = chip * 12 + line % 24 - 12 * k
+        place = (source == iota((4 * lines, width), 1)) & (line % 24 // 12 == k)
+        place_ref[k] = place.astype(bf16)
+
+
 def forward_body(
-    where_ref, own_ref, heads_ref, slots_ref, head_ref, order_ref,
-    z_ref, xp_ref, xm_ref, xa_ref, xb_ref,
-    normed_in_ref, inv_in_ref, active_ref, slope_ref, up_ref, down_ref, normed_out_ref, inv_out_ref, logit_ref,
-    all_ref, total_ref, input_ref,
+    where_ref, own_ref, heads_ref, slots_ref, head_ref, up_ref, down_ref,
+    normed_in_ref, inv_in_ref, active_ref, slope_ref, normed_out_ref, inv_out_ref, logit_ref,
+    total_ref, input_ref,
 ):
     width, lists = own_ref.shape
     samples = slots_ref.shape[1]
     toks = slots_ref.shape[0] // 2
     head = width // toks
-    hidden = z_ref.shape[1]
-    part = z_ref.shape[0]
-    all_ref[0:part] = z_ref[...]
-    all_ref[part : 2 * part] = xp_ref[...]
-    all_ref[2 * part : 3 * part] = xm_ref[...]
-    all_ref[3 * part : 3 * part + part // 2] = xa_ref[...]
-    all_ref[3 * part + part // 2 : 4 * part] = xb_ref[...]
+    hidden = up_ref.shape[1]
     targets = list_targets(slots_ref[0:toks, :], samples // 2)
     row = iota((lists, samples), 0)
     one_own = (row == own_target(targets, where_ref[0])).astype(bf16)
@@ -130,26 +154,18 @@
     inv_in_ref[...] = inverse
     input_ref[...] = jnp.transpose(normed.astype(bf16))
     total_ref[...] = jnp.zeros_like(total_ref)
-    rows = all_ref.shape[0]
-    order_up = (iota((width, rows), 0) == order_ref[0:1, :]).astype(bf16)
-    order_down = (iota((width, rows), 0) == order_ref[1:2, :]).astype(bf16)
     chunk = 256
 
     @pl.loop(0, hidden // chunk)
     def _(i):
         cols = pl.ds(pl.multiple_of(i * chunk, chunk), chunk)
-        block = all_ref[:, cols]
-        up = dot(order_up, block).astype(bf16)
-        down = dot(order_down, block).astype(bf16)
-        up_ref[:, cols] = up
-        down_ref[:, cols] = down
-        pre = dot(input_ref[...], up)
+        pre = dot(input_ref[...], up_ref[:, cols])
         cumulative = 0.5 * (1.0 + lax.erf(pre * (1.0 / math.sqrt(2.0))))
         density = jnp.exp(-0.5 * pre * pre) * (1.0 / math.sqrt(2.0 * math.pi))
         active = (pre * cumulative).astype(bf16)
         active_ref[:, cols] = active
         slope_ref[:, cols] = cumulative + pre * density
-        total_ref[...] += dot(down, active, NT)
+        total_ref[...] += dot(down_ref[:, cols], active, NT)
 
     value = normed_in_ref[...] + total_ref[...]
     centre = jnp.mean(value, axis=0, keepdims=True)
@@ -168,11 +184,10 @@
 
 
 def grad_down_body(
-    chip_ref, logit_ref, slots_ref, head_ref, normed_out_ref, inv_out_ref, active_ref,
+    place_ref, logit_ref, slots_ref, head_ref, normed_out_ref, inv_out_ref, active_ref,
     grad_sum_ref, grad_out_ref, kept_ref, next_ref, far_ref, last_ref, padded_ref,
 ):
     toks = slots_ref.shape[0] // 2
-    width = head_ref.shape[0]
     labels = slots_ref[toks : toks + 1, :].astype(f32)
     dlogit = jax.nn.sigmoid(logit_ref[...]) - labels
     grad = norm_back(dlogit * head_ref[...], normed_out_ref[...], inv_out_ref[...])
@@ -180,15 +195,8 @@
     rounded = grad.astype(bf16)
     grad_out_ref[...] = jnp.transpose(rounded)
     lines, half = kept_ref.shape
-    n_z = lines // 24
-    line = iota((4 * lines, width), 0)
-    chip_x = chip_ref[0] + line // lines
-    chip_z = chip_ref[1] + line % lines // 24
-    chip = chip_x % 4 * n_z + chip_z % n_z
     for k in range(2):
-        source = chip * 12 + line % 24 - 12 * k
-        place = (source == iota((4 * lines, width), 1)) & (line % 24 // 12 == k)
-        padded_ref[k] = dot(place.astype(bf16), rounded).astype(bf16)
+        padded_ref[k] = dot(place_ref[k], rounded).astype(bf16)
     chunk = 256
 
     @pl.loop(0, half // chunk)
@@ -276,8 +284,8 @@
     block = part // n_z
     third = block // 4
     line = np.arange(4 * part)
-    section = line // part
-    step_x = np.array([0, -1, 1, 2])[section]
+    section = np.maximum(line // (part // 2) - 1, 0)
+    step_x = np.array([0, -1, -1, 1, 1, 2, 2])[section]
     step_z = np.asarray(steps_z)[(line % part) // block]
     inner = line % block
     other = inner // (2 * third)
@@ -329,44 +337,57 @@
     line = jnp.concatenate([three, far_before, far_after], axis=0)
     steps_z = (-1, 0, 1, -4, -3, -2, 2, 3)
     part = line.shape[0]
-    x_before, x_after = ring(line, "x", n_x, 1), ring(line, "x", n_x, -1)
-    far_a = ring(x_before[: part // 2], "x", n_x, 1)
-    far_b = ring(x_after[part // 2 :], "x", n_x, -1)
+    half = part // 2
+    lower, upper = line[:half], line[half:]
+    before_a, after_b = ring(lower, "x", n_x, 1), ring(upper, "x", n_x, -1)
+    before_b, after_a = ring(upper, "x", n_x, 1), ring(lower, "x", n_x, -1)
+    far_a, far_b = ring(before_a, "x", n_x, 1), ring(after_b, "x", n_x, -1)
     order = weight_order(lax.axis_index("x"), lax.axis_index("z"), core, n_x, n_z, steps_z, part)
+    third = width // (n_x * n_z * 2)
+    lines = n_z * 4 * third
+    chip = jnp.stack([lax.axis_index("x"), lax.axis_index("z")]).astype(i32)
+    up, down, place = pl.pallas_call(
+        order_body,
+        out_shape=(sds((width, hidden), bf16), sds((width, hidden), bf16), sds((2, n_x * lines, width), bf16)),
+        in_specs=[VM, SM] + [VM] * 7,
+        out_specs=(VM, VM, VM),
+        scratch_shapes=[pltpu.VMEM((4 * part, hidden), bf16)],
+        compiler_params=pltpu.CompilerParams(vmem_limit_bytes=40 * 2**20),
+        cost_estimate=pl.CostEstimate(flops=2 * 10**9, bytes_accessed=8 * 10**6, transcendentals=0),
+        name="order",
+    )(order, chip, line, before_a, before_b, after_a, after_b, far_a, far_b)
 
     where = token.reshape(1).astype(i32)
     head_weight = jnp.where(core == 0, out_weight[0], out_weight[1])[:, None]
     full = (samples, hidden)
-    normed_in, inv_in, active, slope, up, down, normed_out, inv_out, partial = call(
+    normed_in, inv_in, active, slope, normed_out, inv_out, partial = call(
         forward_body,
         (
-            sds((width, samples)), sds((1, samples)), sds(full, bf16), sds(full), sds((width, hidden), bf16),
-            sds((width, hidden), bf16), sds((width, samples)), sds((1, samples)), sds((1, samples)),
+            sds((width, samples)), sds((1, samples)), sds(full, bf16), sds(full),
+            sds((width, samples)), sds((1, samples)), sds((1, samples)),
         ),
-        scratch=(
-            pltpu.VMEM((4 * part, hidden), bf16), pltpu.VMEM((width, samples), f32), pltpu.VMEM((samples, width), bf16)
-        ),
-        n_in=11, smem=1, flops=4 * 10**9, nbytes=10**7,
-    )(where, own, heads, slots, head_weight, order, line, x_before, x_after, far_a, far_b)
+        scratch=(pltpu.VMEM((width, samples), f32), pltpu.VMEM((samples, width), bf16)),
+        n_in=7, smem=1, flops=3 * 10**9, nbytes=8 * 10**6,
+    )(where, own, heads, slots, head_weight, up, down)
     logits = partial + flip(partial, "core", 2, 1)
     there = [flip(logits, "tok", n_tok, k) for k in (1, 2, 3)]
     logits = (logits + there[0]) + (there[1] + there[2])
 
-    third = width // (n_x * n_z * 2)
-    lines = n_z * 4 * third
     block = (lines, hidden // 2)
-    chip = jnp.stack([lax.axis_index("x"), lax.axis_index("z")]).astype(i32)
     grad_sum, grad_out, kept, *away = call(
         grad_down_body,
         (sds((width, samples)), sds((samples, width), bf16), sds(block), sds(block, bf16), sds(block, bf16), sds(block, bf16)),
         scratch=(pltpu.VMEM((2, n_x * lines, samples), bf16),),
-        n_in=7, smem=1, flops=10**9, nbytes=4 * 10**6,
-    )(chip, logits, slots, head_weight, normed_out, inv_out, active)
+        n_in=7, flops=2 * 10**9, nbytes=5 * 10**6,
+    )(place, logits, slots, head_weight, normed_out, inv_out, active)
     come = [ring(v, "x", n_x, k + 1) for k, v in enumerate(away)]
+    pair = 8 * third
     total = kept + sum(v.astype(f32) for v in come)
-    total = [total[k * 4 * third : (k + 1) * 4 * third] for k in range(n_z)]
-    for k in range(1, n_z):
-        total[k] = ring(total[k], "z", n_z, k)
+    total = [total[k * pair : (k + 1) * pair] for k in range(n_z // 2)]
+    total[1:] = [flip(v, "z", n_z, k + 1) for k, v in enumerate(total[1:])]
+    total = (total[0] + total[1]) + (total[2] + total[3])
+    stay, leave = total[: pair // 2], total[pair // 2 :]
+    summed = stay + flip(leave, "z", n_z, n_z // 2)
 
     own_grads, head_grads = call(
         grad_rows_body,
@@ -383,7 +404,6 @@
         n_in=7, smem=1, flops=10**9, nbytes=3 * 10**6,
     )(step_now, row_table, row_accum, last_step, ids, row_counts[:, 0], back.reshape(lists, width))
 
-    summed = sum(total[1:], total[0])
     summed = jnp.concatenate([summed[: 2 * third], summed[2 * third :]], axis=1)
     low, high = summed[:third], summed[third:]
     stay, leave = jnp.where(core == 0, low, high), jnp.where(core == 0, high, low)

time: 141 us -> 161 us (1.14)
  waiting for transfers between devices: 40.2 us -> 62.2 us
  starting transfers between devices: 61.5 us -> 57.6 us
    ppermute x18 -> x13, waiting for transfers between devices: 16.7 us -> 40.8 us  [ring(): lax.ppermute(value, axis, [(i, (i + shift) % size) for i in range(size)])]
    ppermute x18 -> x13, starting transfers between devices: 36.2 us -> 19.5 us  [ring(): lax.ppermute(value, axis, [(i, (i + shift) % size) for i in range(size)])]
    all_to_all x1, waiting for transfers between devices: 7.54 us -> 0.01 us  [on_device(): got = lax.all_to_all(sent, ('x', 'z', 'core'), 0, 0, tiled=True)]
    ppermute x7 -> x11, starting transfers between devices: 4.48 us -> 11.7 us  [flip(): return lax.ppermute(value, axis, [(i, i ^ bit) for i in range(size)])]
    all_to_all x1, starting transfers between devices: 6.37 us -> 12 us  [on_device(): got = lax.all_to_all(sent, ('x', 'z', 'core'), 0, 0, tiled=True)]
    pallas_call x0 -> x1, Pallas kernels: none -> 5.47 us  [on_device(): pl.pallas_call(order_body, out_shape=(sds((width, hidden), bf16), sds((wi...]
    all_to_all x1, waiting for transfers between devices: 0.01 us -> 4.34 us  [on_device(): lax.all_to_all(head_grads.reshape(toks, head, lists), ('tok', 'core'), 0,...]
    pallas_call x1, Pallas kernels: 9 us -> 6.38 us  [on_device(): call(forward_body, (sds((width, samples)), sds((1, samples)), sds(full, b...]
  transfers between devices with their start and end apart: 29 -> 28, of which waited for: 15 -> 16; matrix products, arithmetic and copies ran while one was open for 5% -> 5% of each run, Pallas kernels for 6% -> 5%
where the time goes in v1:
time: 161 us; the launch traced here: 158 us
  waiting for transfers between devices  62.2 us (39%)
  starting transfers between devices  57.6 us (36%)
  Pallas kernels  25 us (16%)
  local copies, waits for them, and re-layouts  8.25 us (5%)
  other arithmetic  3.55 us (2%)
  between operations  1.83 us (1%)
    ppermute x13, waiting for transfers between devices, ring(): lax.ppermute(value, axis, [(i, (i + shift) % size) for i in range(size)])  40.8 us
    ppermute x13, starting transfers between devices, ring(): lax.ppermute(value, axis, [(i, (i + shift) % size) for i in range(size)])  19.5 us
    all_to_all x1, starting transfers between devices, on_device(): got = lax.all_to_all(sent, ('x', 'z', 'core'), 0, 0, tiled=True)  12 us
    ppermute x11, starting transfers between devices, flip(): return lax.ppermute(value, axis, [(i, i ^ bit) for i in range(size)])  11.7 us
    all_to_all x1, waiting for transfers between devices, on_device(): lax.all_to_all(list_grads.reshape(groups, 2 * capacity, width), ('x', 'z'...  8.24 us
    pallas_call x1, Pallas kernels, on_device(): call(grad_rows_body, (sds((width, lists)), sds((width, lists), bf16)), sc...  6.52 us
    all_to_all x1, starting transfers between devices, on_device(): lax.all_to_all(list_grads.reshape(groups, 2 * capacity, width), ('x', 'z'...  6.5 us
    pallas_call x1, Pallas kernels, on_device(): call(forward_body, (sds((width, samples)), sds((1, samples)), sds(full, b...  6.38 us
  transfers between devices with their start and end apart: 28, of which 16 were waited for; matrix products, arithmetic and copies ran while one was open for 5% of the time, Pallas kernels for 5%

profile of v1, /device:TPU:2, one launch (start us, length us, event | category | flops | bytes accessed | tf_op | source)
XLA Modules:
  0.0 158.4 jit_solution(6998194638211341166)
XLA Ops:
  0.6 0.7 pad_add_fusion
  1.4 0.8 copy.27
  2.2 0.8 copy.28
  4.2 1.1 copy-done
  5.3 0.7 copy-done.3
  6.0 0.7 copy-done.5
  6.7 1.3 shard_map.201
  8.2 0.7 reshape.65
  8.9 12.0 %all-to-all-start = ((f16[64,4,384]{2,1,0:T(4,128)(2,1)}), f16[64,4,384]{2,1,0:T(4,128)(2,1)S(1)}, u32[]{:S(2)}, u32[]{:S(2)}) async-start(f16[64,4,384]{2,1,0:T(4,128)(2,1)} %reshape.65), calls=%async_computation | async-start | bytes 393216 | tf_op jit(solution)/shard_map/all_to_all | solution.py:319
  21.0 1.5 collective-permute-start.2
  22.6 1.9 %collective-permute-start.3 = (bf16[24,1536]{1,0:T(8,128)(2,1)S(1)}, bf16[24,1536]{1,0:T(8,128)(2,1)S(1)}, u32[]{:S(2)}, u32[]{:S(2)}) collective-permute-start(bf16[24,1536]{1,0:T(8,128)(2,1)S(1)} %pad_maximum_fusion.3), channel_id=1, source_target_pairs={{0,14},{2,0},{4,2},{6,4},{8,6},{10,8},{12,10},{14,12},{1,15},{3,1}... | collective-permute-start | bytes 221192 | tf_op jit(solution)/shard_map/ppermute | solution.py:276
  24.5 5.6 %collective-permute-done.2 = bf16[24,1536]{1,0:T(8,128)(2,1)S(1)} collective-permute-done((bf16[24,1536]{1,0:T(8,128)(2,1)S(1)}, bf16[24,1536]{1,0:T(8,128)(2,1)S(1)}, u32[]{:S(2)}, u32[]{:S(2)}) %collective-permute-start.2) | collective-permute-done | bytes 73760 | tf_op jit(solution)/shard_map/ppermute | solution.py:276
  30.2 3.5 %collective-permute-start.5 = (bf16[48,1536]{1,0:T(8,128)(2,1)S(1)}, bf16[48,1536]{1,0:T(8,128)(2,1)S(1)}, u32[]{:S(2)}, u32[]{:S(2)}) collective-permute-start(bf16[48,1536]{1,0:T(8,128)(2,1)S(1)} %pad_maximum_fusion.2), channel_id=1, source_target_pairs={{0,10},{2,12},{4,14},{6,0},{8,2},{10,4},{12,6},{14,8},{1,11},{3,13... | collective-permute-start | bytes 442376 | tf_op jit(solution)/shard_map/ppermute | solution.py:276
  34.2 8.8 %collective-permute-done.5 = bf16[48,1536]{1,0:T(8,128)(2,1)S(1)} collective-permute-done((bf16[48,1536]{1,0:T(8,128)(2,1)S(1)}, bf16[48,1536]{1,0:T(8,128)(2,1)S(1)}, u32[]{:S(2)}, u32[]{:S(2)}) %collective-permute-start.5) | collective-permute-done | bytes 147488 | tf_op jit(solution)/shard_map/ppermute | solution.py:276
  42.9 8.6 %collective-permute-done.4 = bf16[72,1536]{1,0:T(8,128)(2,1)S(1)} collective-permute-done((bf16[72,1536]{1,0:T(8,128)(2,1)S(1)}, bf16[72,1536]{1,0:T(8,128)(2,1)S(1)}, u32[]{:S(2)}, u32[]{:S(2)}) %collective-permute-start.4) | collective-permute-done | bytes 221216 | tf_op jit(solution)/shard_map/ppermute | solution.py:276
  51.5 0.7 pad_maximum_fusion
  53.0 1.7 %collective-permute-start.6 = (bf16[96,1536]{1,0:T(8,128)(2,1)S(1)}, bf16[96,1536]{1,0:T(8,128)(2,1)S(1)}, u32[]{:S(2)}, u32[]{:S(2)}) collective-permute-start(bf16[96,1536]{1,0:T(8,128)(2,1)S(1)} %slice.78), channel_id=1, source_target_pairs={{0,16},{16,32},{32,48},{48,0},{1,17},{17,33},{33,49},{49,1},{2,18}... | collective-permute-start | bytes 884744 | tf_op jit(solution)/shard_map/ppermute | solution.py:276
  54.9 1.6 %collective-permute-start.7 = (bf16[96,1536]{1,0:T(8,128)(2,1)}, bf16[96,1536]{1,0:T(8,128)(2,1)S(1)}, u32[]{:S(2)}, u32[]{:S(2)}) collective-permute-start(bf16[96,1536]{1,0:T(8,128)(2,1)} %pad_maximum_fusion), channel_id=1, source_target_pairs={{0,16},{16,32},{32,48},{48,0},{1,17},{17,33},{33,49},{49,1},{2,18}... | collective-permute-start | bytes 884744 | tf_op jit(solution)/shard_map/ppermute | solution.py:276
  57.5 0.9 copy.29
  58.3 4.5 %all-to-all-start.1 = ((f16[8,48,256]{2,1,0:T(8,128)(2,1)}), f16[8,48,256]{2,1,0:T(8,128)(2,1)S(1)}, u32[]{:S(2)}, u32[]{:S(2)}) async-start(f16[8,48,256]{2,1,0:T(8,128)(2,1)} %bitcast.13), calls=%async_computation.1 | async-start | bytes 393216 | tf_op jit(solution)/shard_map/all_to_all | solution.py:321
  62.8 2.8 %collective-permute-start.11 = (bf16[96,1536]{1,0:T(8,128)(2,1)S(1)}, bf16[96,1536]{1,0:T(8,128)(2,1)S(1)}, u32[]{:S(2)}, u32[]{:S(2)}) collective-permute-start(bf16[96,1536]{1,0:T(8,128)(2,1)S(1)} %collective-permute-done.9.xd_ref), channel_id=1, source_target_pairs={{0,48},{16,0},{32,16},{48,32},{1,49},{17,1},{33,17},{49,33},{2,50}... | collective-permute-start | bytes 884744 | tf_op jit(solution)/shard_map/ppermute | solution.py:276
  65.6 1.0 bitcast_convert_fusion.1.own_ref
  66.5 3.0 %all-to-all-done.1 = f16[8,48,256]{2,1,0:T(8,128)(2,1)S(1)} async-done(((f16[8,48,256]{2,1,0:T(8,128)(2,1)}), f16[8,48,256]{2,1,0:T(8,128)(2,1)S(1)}, u32[]{:S(2)}, u32[]{:S(2)}) %all-to-all-start.1) | async-done | bytes 196640 | tf_op jit(solution)/shard_map/all_to_all | solution.py:321
  70.0 4.0 %collective-permute-done.11.xf_ref = bf16[96,1536]{1,0:T(8,128)(2,1)S(1)} collective-permute-done((bf16[96,1536]{1,0:T(8,128)(2,1)S(1)}, bf16[96,1536]{1,0:T(8,128)(2,1)S(1)}, u32[]{:S(2)}, u32[]{:S(2)}) %collective-permute-start.11) | collective-permute-done | bytes 294944 | tf_op jit(solution)/shard_map/ppermute | solution.py:276
  74.0 1.6 collective-permute-done.10.xe_ref
  75.6 5.5 %order.1 = (bf16[384,1536]{1,0:T(8,128)(2,1)S(1)}, bf16[384,1536]{1,0:T(8,128)(2,1)S(1)}, bf16[2,768,384]{2,1,0:T(8,128)(2,1)S(1)}) custom-call(s32[2,768]{1,0:T(2,128)S(1)} %pad_add_fusion.1.order_ref, s32[2]{0:T(128)S(1)} %pad_add_fusion.2.chip_ref, bf16[192,1536]{1,0:T(8,128)(2,1)S(1)} %concatenate.43.z_ref, ...), custom_call_target="tpu_custom_call" | custom-call | flops 2000000000 | bytes 8000000 | tf_op jit(solution)/shard_map/order/pallas_call | solution.py:349
  81.1 6.4 %shard_map.202 = (f32[384,512]{1,0:T(8,128)S(1)}, f32[1,512]{1,0:T(1,128)S(1)}, bf16[512,1536]{1,0:T(8,128)(2,1)S(1)}, f32[512,1536]{1,0:T(8,128)S(1)}, f32[384,...) custom-call(s32[1]{0:T(128)} %bitcast.4.where_ref, f32[384,256]{1,0:T(8,128)S(1)} %bitcast_convert_fusion.1.own_ref, ...), custom_call_target="tpu_custom_call" | custom-call | flops 3000000000 | bytes 8000000 | tf_op jit(solution)/shard_map/pallas_call | solution.py:363
  87.6 1.1 collective-permute-done.12
  88.7 3.0 %collective-permute-start.15 = (f32[1,512]{1,0:T(1,128)S(1)}, f32[1,512]{1,0:T(1,128)S(1)}, u32[]{:S(2)}, u32[]{:S(2)}) collective-permute-start(f32[1,512]{1,0:T(1,128)S(1)} %add.92), channel_id=1, source_target_pairs={{0,192},{64,128},{128,64},{192,0},{1,193},{65,129},{129,65},{193,1... | collective-permute-start | bytes 6152 | tf_op jit(solution)/shard_map/ppermute | solution.py:280
  91.7 0.6 collective-permute-start.14
  92.8 0.7 collective-permute-done.15
  93.5 3.3 %collective-permute-done.14 = f32[1,512]{1,0:T(1,128)S(1)} collective-permute-done((f32[1,512]{1,0:T(1,128)S(1)}, f32[1,512]{1,0:T(1,128)S(1)}, u32[]{:S(2)}, u32[]{:S(2)}) %collective-permute-start.14) | collective-permute-done | bytes 2080 | tf_op jit(solution)/shard_map/ppermute | solution.py:280
  96.8 3.0 %shard_map.203 = (f32[384,512]{1,0:T(8,128)S(1)}, bf16[512,384]{1,0:T(8,128)(2,1)S(1)}, f32[192,768]{1,0:T(8,128)S(1)}, bf16[192,768]{1,0:T(8,128)(2,1)S(1)}, bf...) custom-call(bf16[2,768,384]{2,1,0:T(8,128)(2,1)S(1)} %get-tuple-element.24.place_ref, ...), custom_call_target="tpu_custom_call" | custom-call | flops 2000000000 | bytes 5000000 | tf_op jit(solution)/shard_map/pallas_call | solution.py:377
  100.3 4.7 %collective-permute-start.17 = (bf16[192,768]{1,0:T(8,128)(2,1)S(1)}, bf16[192,768]{1,0:T(8,128)(2,1)S(1)}, u32[]{:S(2)}, u32[]{:S(2)}) collective-permute-start(bf16[192,768]{1,0:T(8,128)(2,1)S(1)} %get-tuple-element.42), channel_id=1, source_target_pairs={{0,32},{16,48},{32,0},{48,16},{1,33},{17,49},{33,1},{49,17},{2,34}... | collective-permute-start | bytes 884744 | tf_op jit(solution)/shard_map/ppermute | solution.py:276
  105.0 5.8 %collective-permute-done.16 = bf16[192,768]{1,0:T(8,128)(2,1)S(1)} collective-permute-done((bf16[192,768]{1,0:T(8,128)(2,1)S(1)}, bf16[192,768]{1,0:T(8,128)(2,1)S(1)}, u32[]{:S(2)}, u32[]{:S(2)}) %collective-permute-start.16) | collective-permute-done | bytes 294944 | tf_op jit(solution)/shard_map/ppermute | solution.py:276
  110.8 2.1 %collective-permute-done.17 = bf16[192,768]{1,0:T(8,128)(2,1)S(1)} collective-permute-done((bf16[192,768]{1,0:T(8,128)(2,1)S(1)}, bf16[192,768]{1,0:T(8,128)(2,1)S(1)}, u32[]{:S(2)}, u32[]{:S(2)}) %collective-permute-start.17) | collective-permute-done | bytes 294944 | tf_op jit(solution)/shard_map/ppermute | solution.py:276
  112.9 4.0 %collective-permute-done.18 = bf16[192,768]{1,0:T(8,128)(2,1)S(1)} collective-permute-done((bf16[192,768]{1,0:T(8,128)(2,1)S(1)}, bf16[192,768]{1,0:T(8,128)(2,1)S(1)}, u32[]{:S(2)}, u32[]{:S(2)}) %collective-permute-start.18) | collective-permute-done | bytes 294944 | tf_op jit(solution)/shard_map/ppermute | solution.py:276
  117.2 0.9 collective-permute-start.20
  118.1 3.5 %collective-permute-start.19 = (f32[48,768]{1,0:T(8,128)S(1)}, f32[48,768]{1,0:T(8,128)S(1)}, u32[]{:S(2)}, u32[]{:S(2)}) collective-permute-start(f32[48,768]{1,0:T(8,128)S(1)} %get-tuple-element.54), channel_id=1, source_target_pairs={{0,2},{2,0},{4,6},{6,4},{8,10},{10,8},{12,14},{14,12},{1,3},{3,1},... | collective-permute-start | bytes 442376 | tf_op jit(solution)/shard_map/ppermute | solution.py:280
  121.6 6.5 %shard_map.204 = (f32[384,256]{1,0:T(8,128)S(1)}, bf16[384,256]{1,0:T(8,128)(2,1)}) custom-call(s32[1]{0:T(128)} %bitcast.4.where_ref, s32[16,512]{1,0:T(8,128)S(1)} %add_select_fusion.slots_ref, f32[384,512]{1,0:T(8,128)S(1)} %get-tuple-element.31.grad_sum_ref, bf16[512,384]{1,0:T(8,128)(2,1)S(1)} %get-tuple-element.32.grad_out_ref, ...), custom_call_target="tpu_custom_call" | custom-call | flops 2000000000 | bytes 8000000 | tf_op jit(solution)/shard_map/pallas_call | solution.py:392
  128.1 3.4 %all-to-all-start.2 = ((bf16[8,48,256]{2,1,0:T(8,128)(2,1)}), bf16[8,48,256]{2,1,0:T(8,128)(2,1)S(1)}, u32[]{:S(2)}, u32[]{:S(2)}) async-start(bf16[8,48,256]{2,1,0:T(8,128)(2,1)} %bitcast.16), calls=%async_computation.2 | async-start | bytes 393216 | tf_op jit(solution)/shard_map/all_to_all | solution.py:398
  131.6 2.3 %collective-permute-start.22 = (f32[24,768]{1,0:T(8,128)S(1)}, f32[24,768]{1,0:T(8,128)S(1)}, u32[]{:S(2)}, u32[]{:S(2)}) collective-permute-start(f32[24,768]{1,0:T(8,128)S(1)} %slice.84), channel_id=1, source_target_pairs={{0,8},{2,10},{4,12},{6,14},{8,0},{10,2},{12,4},{14,6},{1,9},{3,11}... | collective-permute-start | bytes 221192 | tf_op jit(solution)/shard_map/ppermute | solution.py:280
  133.9 4.3 %all-to-all-done.2 = bf16[8,48,256]{2,1,0:T(8,128)(2,1)S(1)} async-done(((bf16[8,48,256]{2,1,0:T(8,128)(2,1)}), bf16[8,48,256]{2,1,0:T(8,128)(2,1)S(1)}, u32[]{:S(2)}, u32[]{:S(2)}) %all-to-all-start.2) | async-done | bytes 196640 | tf_op jit(solution)/shard_map/all_to_all | solution.py:398
  138.5 0.7 reshape.69
  139.2 6.5 %all-to-all-start.3 = ((bf16[64,4,384]{2,1,0:T(4,128)(2,1)}), bf16[64,4,384]{2,1,0:T(4,128)(2,1)S(1)}, u32[]{:S(2)}, u32[]{:S(2)}) async-start(bf16[64,4,384]{2,1,0:T(4,128)(2,1)} %reshape.69), calls=%async_computation.3 | async-start | bytes 393216 | tf_op jit(solution)/shard_map/all_to_all | solution.py:400
  147.1 0.7 copy.33
  147.8 8.2 %all-to-all-done.3 = bf16[64,4,384]{2,1,0:T(4,128)(2,1)S(1)} async-done(((bf16[64,4,384]{2,1,0:T(4,128)(2,1)}), bf16[64,4,384]{2,1,0:T(4,128)(2,1)S(1)}, u32[]{:S(2)}, u32[]{:S(2)}) %all-to-all-start.3) | async-done | bytes 196640 | tf_op jit(solution)/shard_map/all_to_all | solution.py:400
  156.2 2.2 %shard_map.205 = (f32[2,256,384]{2,1,0:T(8,128)}, f32[2,256]{1,0:T(2,128)}) custom-call(s32[1]{0:T(128)S(6)} %copy.34.step_ref, f32[2,256,384]{2,1,0:T(8,128)S(1)} %copy-done.1, f32[2,256]{1,0:T(2,128)S(1)} %copy-done.2, s32[2,256]{1,0:T(2,128)S(1)} %copy-done.4, s32[4,64]{1,0:T(4,128)S(1)} %bitcast.34, s32[2,64]{1,0:T(2,128)S(1)} %bitcast.35, ...), custom_call_target="tpu_custom_call" | custom-call | flops 1000000000 | bytes 3000000 | tf_op jit(solution)/shard_map/pallas_call | solution.py:401
  (92 shorter events, 6.6 us)
Async XLA Ops:
  1.4 53.5 %collective-permute-start = (s32[16,256]{1,0:T(8,128)S(1)}, s32[16,256]{1,0:T(8,128)S(1)}, u32[]{:S(2)}, u32[]{:S(2)}) collective-permute-start(s32[16,256]{1,0:T(8,128)S(1)} %pad_add_fusion), channel_id=1, source_target_pairs={{0,1},{1,0},{2,3},{3,2},{4,5},{5,4},{6,7},{7,6},{8,9},{9,8},{10,11... | collective-permute-start | bytes 49160 | tf_op jit(solution)/shard_map/ppermute | solution.py:280
  3.0 18.0 %collective-permute-start.1 = (bf16[12,1536]{1,0:T(8,128)(2,1)S(1)}, bf16[12,1536]{1,0:T(8,128)(2,1)S(1)}, u32[]{:S(2)}, u32[]{:S(2)}) collective-permute-start(bf16[12,1536]{1,0:T(8,128)(2,1)S(1)} %get-tuple-element.58), channel_id=1, source_target_pairs={{0,1},{1,0},{2,3},{3,2},{4,5},{5,4},{6,7},{7,6},{8,9},{9,8},{10,11... | collective-permute-start | bytes 110600 | tf_op jit(solution)/shard_map/ppermute | solution.py:280
  4.2 1.1 copy-start
  5.3 0.7 copy-start.3
  6.0 0.7 copy-start.5
  8.1 14.5 %copy-start.10 = (s32[768]{0:T(1024)S(1)}, s32[768]{0:T(1024)}, u32[]{:S(2)}) copy-start(s32[768]{0:T(1024)} %constant.73.clone) | copy-start | bytes 9220
  8.1 14.5 %copy-start.11 = (s32[768]{0:T(1024)S(1)}, s32[768]{0:T(1024)}, u32[]{:S(2)}) copy-start(s32[768]{0:T(1024)} %constant.72.clone) | copy-start | bytes 9220
  8.1 14.5 %copy-start.12 = (s32[768]{0:T(1024)S(1)}, s32[768]{0:T(1024)}, u32[]{:S(2)}) copy-start(s32[768]{0:T(1024)} %constant.71.clone) | copy-start | bytes 9220
  8.1 14.5 %copy-start.13 = (s32[768]{0:T(1024)S(1)}, s32[768]{0:T(1024)}, u32[]{:S(2)}) copy-start(s32[768]{0:T(1024)} %constant.70.clone) | copy-start | bytes 9220
  8.1 14.5 %copy-start.14 = (s32[768]{0:T(1024)S(1)}, s32[768]{0:T(1024)}, u32[]{:S(2)}) copy-start(s32[768]{0:T(1024)} %constant.69.clone) | copy-start | bytes 9220
  8.1 14.5 %copy-start.16 = (pred[768]{0:T(1024)(128)(4,1)S(1)}, pred[768]{0:T(1024)(128)(4,1)}, u32[]{:S(2)}) copy-start(pred[768]{0:T(1024)(128)(4,1)} %constant.75.clone) | copy-start | bytes 2308
  8.1 14.5 %copy-start.17 = (pred[768]{0:T(1024)(128)(4,1)S(1)}, pred[768]{0:T(1024)(128)(4,1)}, u32[]{:S(2)}) copy-start(pred[768]{0:T(1024)(128)(4,1)} %constant.74.clone) | copy-start | bytes 2308
  8.1 26.0 %copy-start.15 = (f32[2,384]{1,0:T(2,128)S(1)}, f32[2,384]{1,0:T(2,128)}, u32[]{:S(2)}) copy-start(f32[2,384]{1,0:T(2,128)} %param.28) | copy-start | bytes 9220
  8.9 48.5 %all-to-all-start = ((f16[64,4,384]{2,1,0:T(4,128)(2,1)}), f16[64,4,384]{2,1,0:T(4,128)(2,1)S(1)}, u32[]{:S(2)}, u32[]{:S(2)}) async-start(f16[64,4,384]{2,1,0:T(4,128)(2,1)} %reshape.65), calls=%async_computation | async-start | bytes 393216 | tf_op jit(solution)/shard_map/all_to_all | solution.py:319
  21.0 9.1 %collective-permute-start.2 = (bf16[24,1536]{1,0:T(8,128)(2,1)S(1)}, bf16[24,1536]{1,0:T(8,128)(2,1)S(1)}, u32[]{:S(2)}, u32[]{:S(2)}) collective-permute-start(bf16[24,1536]{1,0:T(8,128)(2,1)S(1)} %pad_maximum_fusion.3), channel_id=1, source_target_pairs={{0,2},{2,4},{4,6},{6,8},{8,10},{10,12},{12,14},{14,0},{1,3},{3,5},... | collective-permute-start | bytes 221192 | tf_op jit(solution)/shard_map/ppermute | solution.py:276
  22.6 11.0 %collective-permute-start.3 = (bf16[24,1536]{1,0:T(8,128)(2,1)S(1)}, bf16[24,1536]{1,0:T(8,128)(2,1)S(1)}, u32[]{:S(2)}, u32[]{:S(2)}) collective-permute-start(bf16[24,1536]{1,0:T(8,128)(2,1)S(1)} %pad_maximum_fusion.3), channel_id=1, source_target_pairs={{0,14},{2,0},{4,2},{6,4},{8,6},{10,8},{12,10},{14,12},{1,15},{3,1}... | collective-permute-start | bytes 221192 | tf_op jit(solution)/shard_map/ppermute | solution.py:276
  30.2 12.8 %collective-permute-start.5 = (bf16[48,1536]{1,0:T(8,128)(2,1)S(1)}, bf16[48,1536]{1,0:T(8,128)(2,1)S(1)}, u32[]{:S(2)}, u32[]{:S(2)}) collective-permute-start(bf16[48,1536]{1,0:T(8,128)(2,1)S(1)} %pad_maximum_fusion.2), channel_id=1, source_target_pairs={{0,10},{2,12},{4,14},{6,0},{8,2},{10,4},{12,6},{14,8},{1,11},{3,13... | collective-permute-start | bytes 442376 | tf_op jit(solution)/shard_map/ppermute | solution.py:276
  33.7 17.8 %collective-permute-start.4 = (bf16[72,1536]{1,0:T(8,128)(2,1)S(1)}, bf16[72,1536]{1,0:T(8,128)(2,1)S(1)}, u32[]{:S(2)}, u32[]{:S(2)}) collective-permute-start(bf16[72,1536]{1,0:T(8,128)(2,1)S(1)} %pad_maximum_fusion.1), channel_id=1, source_target_pairs={{0,6},{2,8},{4,10},{6,12},{8,14},{10,0},{12,2},{14,4},{1,7},{3,9},... | collective-permute-start | bytes 663560 | tf_op jit(solution)/shard_map/ppermute | solution.py:276
  34.2 20.7 %copy-start.8 = (s32[8,256]{1,0:T(8,128)S(1)}, s32[8,256]{1,0:T(8,128)}, u32[]{:S(2)}) copy-start(s32[8,256]{1,0:T(8,128)} %param.24) | copy-start | bytes 24580
  34.2 20.7 %copy-start.9 = (s32[256]{0:T(256)S(1)}, s32[256]{0:T(256)}, u32[]{:S(2)}) copy-start(s32[256]{0:T(256)} %param.25) | copy-start | bytes 3076
  52.2 10.5 %collective-permute-start.9 = (bf16[96,1536]{1,0:T(8,128)(2,1)}, bf16[96,1536]{1,0:T(8,128)(2,1)S(1)}, u32[]{:S(2)}, u32[]{:S(2)}) collective-permute-start(bf16[96,1536]{1,0:T(8,128)(2,1)} %pad_maximum_fusion), channel_id=1, source_target_pairs={{0,48},{16,0},{32,16},{48,32},{1,49},{17,1},{33,17},{49,33},{2,50}... | collective-permute-start | bytes 884744 | tf_op jit(solution)/shard_map/ppermute | solution.py:276
  53.0 12.6 %collective-permute-start.6 = (bf16[96,1536]{1,0:T(8,128)(2,1)S(1)}, bf16[96,1536]{1,0:T(8,128)(2,1)S(1)}, u32[]{:S(2)}, u32[]{:S(2)}) collective-permute-start(bf16[96,1536]{1,0:T(8,128)(2,1)S(1)} %slice.78), channel_id=1, source_target_pairs={{0,16},{16,32},{32,48},{48,0},{1,17},{17,33},{33,49},{49,1},{2,18}... | collective-permute-start | bytes 884744 | tf_op jit(solution)/shard_map/ppermute | solution.py:276
  54.9 15.1 %collective-permute-start.7 = (bf16[96,1536]{1,0:T(8,128)(2,1)}, bf16[96,1536]{1,0:T(8,128)(2,1)S(1)}, u32[]{:S(2)}, u32[]{:S(2)}) collective-permute-start(bf16[96,1536]{1,0:T(8,128)(2,1)} %pad_maximum_fusion), channel_id=1, source_target_pairs={{0,16},{16,32},{32,48},{48,0},{1,17},{17,33},{33,49},{49,1},{2,18}... | collective-permute-start | bytes 884744 | tf_op jit(solution)/shard_map/ppermute | solution.py:276
  56.6 13.5 %collective-permute-start.8 = (bf16[96,1536]{1,0:T(8,128)(2,1)S(1)}, bf16[96,1536]{1,0:T(8,128)(2,1)S(1)}, u32[]{:S(2)}, u32[]{:S(2)}) collective-permute-start(bf16[96,1536]{1,0:T(8,128)(2,1)S(1)} %slice.78), channel_id=1, source_target_pairs={{0,48},{16,0},{32,16},{48,32},{1,49},{17,1},{33,17},{49,33},{2,50}... | collective-permute-start | bytes 884744 | tf_op jit(solution)/shard_map/ppermute | solution.py:276
  58.3 11.3 %all-to-all-start.1 = ((f16[8,48,256]{2,1,0:T(8,128)(2,1)}), f16[8,48,256]{2,1,0:T(8,128)(2,1)S(1)}, u32[]{:S(2)}, u32[]{:S(2)}) async-start(f16[8,48,256]{2,1,0:T(8,128)(2,1)} %bitcast.13), calls=%async_computation.1 | async-start | bytes 393216 | tf_op jit(solution)/shard_map/all_to_all | solution.py:321
  62.8 11.2 %collective-permute-start.11 = (bf16[96,1536]{1,0:T(8,128)(2,1)S(1)}, bf16[96,1536]{1,0:T(8,128)(2,1)S(1)}, u32[]{:S(2)}, u32[]{:S(2)}) collective-permute-start(bf16[96,1536]{1,0:T(8,128)(2,1)S(1)} %collective-permute-done.9.xd_ref), channel_id=1, source_target_pairs={{0,48},{16,0},{32,16},{48,32},{1,49},{17,1},{33,17},{49,33},{2,50}... | collective-permute-start | bytes 884744 | tf_op jit(solution)/shard_map/ppermute | solution.py:276
  65.6 10.0 %collective-permute-start.10 = (bf16[96,1536]{1,0:T(8,128)(2,1)S(1)}, bf16[96,1536]{1,0:T(8,128)(2,1)S(1)}, u32[]{:S(2)}, u32[]{:S(2)}) collective-permute-start(bf16[96,1536]{1,0:T(8,128)(2,1)S(1)} %collective-permute-done.6.xa_ref), channel_id=1, source_target_pairs={{0,16},{16,32},{32,48},{48,0},{1,17},{17,33},{33,49},{49,1},{2,18}... | collective-permute-start | bytes 884744 | tf_op jit(solution)/shard_map/ppermute | solution.py:276
  87.5 1.3 collective-permute-start.12
  88.7 4.8 %collective-permute-start.15 = (f32[1,512]{1,0:T(1,128)S(1)}, f32[1,512]{1,0:T(1,128)S(1)}, u32[]{:S(2)}, u32[]{:S(2)}) collective-permute-start(f32[1,512]{1,0:T(1,128)S(1)} %add.92), channel_id=1, source_target_pairs={{0,192},{64,128},{128,64},{192,0},{1,193},{65,129},{129,65},{193,1... | collective-permute-start | bytes 6152 | tf_op jit(solution)/shard_map/ppermute | solution.py:280
  91.7 5.1 %collective-permute-start.14 = (f32[1,512]{1,0:T(1,128)S(1)}, f32[1,512]{1,0:T(1,128)S(1)}, u32[]{:S(2)}, u32[]{:S(2)}) collective-permute-start(f32[1,512]{1,0:T(1,128)S(1)} %add.92), channel_id=1, source_target_pairs={{0,128},{64,192},{128,0},{192,64},{1,129},{65,193},{129,1},{193,65... | collective-permute-start | bytes 6152 | tf_op jit(solution)/shard_map/ppermute | solution.py:280
  92.4 4.5 %collective-permute-start.13 = (f32[1,512]{1,0:T(1,128)S(1)}, f32[1,512]{1,0:T(1,128)S(1)}, u32[]{:S(2)}, u32[]{:S(2)}) collective-permute-start(f32[1,512]{1,0:T(1,128)S(1)} %add.92), channel_id=1, source_target_pairs={{0,64},{64,0},{128,192},{192,128},{1,65},{65,1},{129,193},{193,129... | collective-permute-start | bytes 6152 | tf_op jit(solution)/shard_map/ppermute | solution.py:280
  99.9 10.9 %collective-permute-start.16 = (bf16[192,768]{1,0:T(8,128)(2,1)S(1)}, bf16[192,768]{1,0:T(8,128)(2,1)S(1)}, u32[]{:S(2)}, u32[]{:S(2)}) collective-permute-start(bf16[192,768]{1,0:T(8,128)(2,1)S(1)} %get-tuple-element.41), channel_id=1, source_target_pairs={{0,16},{16,32},{32,48},{48,0},{1,17},{17,33},{33,49},{49,1},{2,18}... | collective-permute-start | bytes 884744 | tf_op jit(solution)/shard_map/ppermute | solution.py:276
  100.3 12.6 %collective-permute-start.17 = (bf16[192,768]{1,0:T(8,128)(2,1)S(1)}, bf16[192,768]{1,0:T(8,128)(2,1)S(1)}, u32[]{:S(2)}, u32[]{:S(2)}) collective-permute-start(bf16[192,768]{1,0:T(8,128)(2,1)S(1)} %get-tuple-element.42), channel_id=1, source_target_pairs={{0,32},{16,48},{32,0},{48,16},{1,33},{17,49},{33,1},{49,17},{2,34}... | collective-permute-start | bytes 884744 | tf_op jit(solution)/shard_map/ppermute | solution.py:276
  105.0 11.9 %collective-permute-start.18 = (bf16[192,768]{1,0:T(8,128)(2,1)S(1)}, bf16[192,768]{1,0:T(8,128)(2,1)S(1)}, u32[]{:S(2)}, u32[]{:S(2)}) collective-permute-start(bf16[192,768]{1,0:T(8,128)(2,1)S(1)} %get-tuple-element.43), channel_id=1, source_target_pairs={{0,48},{16,0},{32,16},{48,32},{1,49},{17,1},{33,17},{49,33},{2,50}... | collective-permute-start | bytes 884744 | tf_op jit(solution)/shard_map/ppermute | solution.py:276
  117.1 14.4 %collective-permute-start.21 = (f32[48,768]{1,0:T(8,128)S(1)}, f32[48,768]{1,0:T(8,128)S(1)}, u32[]{:S(2)}, u32[]{:S(2)}) collective-permute-start(f32[48,768]{1,0:T(8,128)S(1)} %get-tuple-element.52), channel_id=1, source_target_pairs={{0,6},{2,4},{4,2},{6,0},{8,14},{10,12},{12,10},{14,8},{1,7},{3,5},... | collective-permute-start | bytes 442376 | tf_op jit(solution)/shard_map/ppermute | solution.py:280
  117.2 14.3 %collective-permute-start.20 = (f32[48,768]{1,0:T(8,128)S(1)}, f32[48,768]{1,0:T(8,128)S(1)}, u32[]{:S(2)}, u32[]{:S(2)}) collective-permute-start(f32[48,768]{1,0:T(8,128)S(1)} %get-tuple-element.53), channel_id=1, source_target_pairs={{0,4},{2,6},{4,0},{6,2},{8,12},{10,14},{12,8},{14,10},{1,5},{3,7},... | collective-permute-start | bytes 442376 | tf_op jit(solution)/shard_map/ppermute | solution.py:280
  118.1 13.5 %collective-permute-start.19 = (f32[48,768]{1,0:T(8,128)S(1)}, f32[48,768]{1,0:T(8,128)S(1)}, u32[]{:S(2)}, u32[]{:S(2)}) collective-permute-start(f32[48,768]{1,0:T(8,128)S(1)} %get-tuple-element.54), channel_id=1, source_target_pairs={{0,2},{2,0},{4,6},{6,4},{8,10},{10,8},{12,14},{14,12},{1,3},{3,1},... | collective-permute-start | bytes 442376 | tf_op jit(solution)/shard_map/ppermute | solution.py:280
  128.1 10.1 %all-to-all-start.2 = ((bf16[8,48,256]{2,1,0:T(8,128)(2,1)}), bf16[8,48,256]{2,1,0:T(8,128)(2,1)S(1)}, u32[]{:S(2)}, u32[]{:S(2)}) async-start(bf16[8,48,256]{2,1,0:T(8,128)(2,1)} %bitcast.16), calls=%async_computation.2 | async-start | bytes 393216 | tf_op jit(solution)/shard_map/all_to_all | solution.py:398
  131.6 14.2 %collective-permute-start.22 = (f32[24,768]{1,0:T(8,128)S(1)}, f32[24,768]{1,0:T(8,128)S(1)}, u32[]{:S(2)}, u32[]{:S(2)}) collective-permute-start(f32[24,768]{1,0:T(8,128)S(1)} %slice.84), channel_id=1, source_target_pairs={{0,8},{2,10},{4,12},{6,14},{8,0},{10,2},{12,4},{14,6},{1,9},{3,11}... | collective-permute-start | bytes 221192 | tf_op jit(solution)/shard_map/ppermute | solution.py:280
  138.4 17.7 %copy-start.1 = (f32[2,256,384]{2,1,0:T(8,128)S(1)}, f32[2,256,384]{2,1,0:T(8,128)}, u32[]{:S(2)}) copy-start(f32[2,256,384]{2,1,0:T(8,128)} %table_ref.3) | copy-start | bytes 2359300
  138.5 17.7 %copy-start.2 = (f32[2,256]{1,0:T(2,128)S(1)}, f32[2,256]{1,0:T(2,128)}, u32[]{:S(2)}) copy-start(f32[2,256]{1,0:T(2,128)} %accum_ref.1) | copy-start | bytes 6148
  138.5 17.7 %copy-start.4 = (s32[2,256]{1,0:T(2,128)S(1)}, s32[2,256]{1,0:T(2,128)}, u32[]{:S(2)}) copy-start(s32[2,256]{1,0:T(2,128)} %last_ref.3) | copy-start | bytes 6148
  138.5 17.7 %copy-start.6 = (s32[2,1,64,2]{2,3,1,0:T(2,128)S(1)}, s32[2,1,64,2]{2,3,1,0:T(2,128)}, u32[]{:S(2)}) copy-start(s32[2,1,64,2]{2,3,1,0:T(2,128)} %param.22) | copy-start | bytes 3076
  138.5 17.7 %copy-start.7 = (s32[2,1,64]{2,1,0:T(1,128)S(1)}, s32[2,1,64]{2,1,0:T(1,128)}, u32[]{:S(2)}) copy-start(s32[2,1,64]{2,1,0:T(1,128)} %param.23) | copy-start | bytes 1540
  139.2 16.8 %all-to-all-start.3 = ((bf16[64,4,384]{2,1,0:T(4,128)(2,1)}), bf16[64,4,384]{2,1,0:T(4,128)(2,1)S(1)}, u32[]{:S(2)}, u32[]{:S(2)}) async-start(bf16[64,4,384]{2,1,0:T(4,128)(2,1)} %reshape.69), calls=%async_computation.3 | async-start | bytes 393216 | tf_op jit(solution)/shard_map/all_to_all | solution.py:400
  145.8 1.3 collective-permute-start.23
